TPU v7x, 128 devices: a whole 4x4x4 slice. The times are simulated.
128 devices in a mesh: ty: 8 (over y, core), tx: 16 (over x, z).
Axes of the slice: x: 4, y: 4, z: 4, core: 2. Of those that a mesh axis runs over, the one named last changes fastest.
Arguments:
- source_fields: float32 [8, 768, 4096], P(None, 'ty', 'tx'), may hold values from -6 to 6
- diffusivity: float32 [768, 4096], P('ty', 'tx'), may hold values from 0.03 to 0.24
- cell_area: float32 [768, 4096], P('ty', 'tx'), may hold values from 0.5 to 2
- pair_block: int32 [32768], P(('ty', 'tx')), may hold values from 0 to 191
- pair_owner: int32 [32768, 1], P(('ty', 'tx')), may hold values from 0 to 127; in each aligned block of 256 rows (0 to 255, 256 to 511, ...) at most 4 rows name the same one
- pair_target: int32 [32768], P(('ty', 'tx')), may hold values from 0 to 15
- weight_blocks: bfloat16 [32768, 128, 128], P(('ty', 'tx')), may hold values from 0.0099487305 to 0.099609375
- target_area: float32 [2048, 128], P(('ty', 'tx')), may hold values from 1 to 4
Outputs:
- regridded: float32 [2048, 8, 128], P(('ty', 'tx'))
Inputs may be any that keep to these rules, and one draw needn't show every extreme that they name: `pair_owner`: among the 256 pairs held by one device, no owner is named more than 4 times; some device names some owner exactly 4 times.
All inputs are finite; a program needn't handle non-finite values.
Results may differ from a plain program's by a relative error of at most 0.0018.
Values sent between devices are 32-bit elements; how exact they have to be, the bound alone decides.
A program may use at most 64 MiB of HBM per device.

v0:
```python
import jax
import jax.numpy as jnp
from jax import lax
from jax.sharding import PartitionSpec as P

NVAR = 8
BH = 8
BW = 16
BR = 12
BCOL = 16
TBD = 16


def padded_2(shard, sides, width):
    for axis, dim in sides:
        peers, length = (lax.axis_size(axis), shard.shape[dim])
        up = [(i, (i + 1) % peers) for i in range(peers)]
        down = [(j, i) for i, j in up]
        last = lax.slice_in_dim(shard, length - width, length, axis=dim)
        initial = lax.slice_in_dim(shard, 0, width, axis=dim)
        before = lax.ppermute(last, axis, up)
        after = lax.ppermute(initial, axis, down)
        shard = jnp.concatenate([before, shard, after], axis=dim)
    return shard


def diffuse(padded, rate_padded, row_start, total_rows):
    centre = padded[:, 1:-1, 1:-1]
    own_rate = rate_padded[1:-1, 1:-1]
    k_east = 0.5 * (own_rate + rate_padded[1:-1, 2:])
    k_west = 0.5 * (own_rate + rate_padded[1:-1, :-2])
    k_north = 0.5 * (own_rate + rate_padded[2:, 1:-1])
    k_south = 0.5 * (own_rate + rate_padded[:-2, 1:-1])
    row_index = row_start + lax.iota(jnp.int32, centre.shape[1])[:, None]
    k_north = jnp.where(row_index < total_rows - 1, k_north, 0.0)
    k_south = jnp.where(row_index > 0, k_south, 0.0)
    return (
        centre
        + k_east * (padded[:, 1:-1, 2:] - centre)
        + k_west * (padded[:, 1:-1, :-2] - centre)
        + k_north * (padded[:, 2:, 1:-1] - centre)
        + k_south * (padded[:, :-2, 1:-1] - centre)
    )


def on_device(
    source_fields,
    diffusivity,
    cell_area,
    pair_block,
    pair_owner,
    pair_target,
    weight_blocks,
    target_area,
):
    row_count = source_fields.shape[1]
    total_rows = row_count * lax.axis_size("ty")
    row_start = lax.axis_index("ty") * row_count
    stacked = jnp.concatenate([source_fields, diffusivity[None]], axis=0)
    padded = padded_2(stacked, (("ty", 1), ("tx", 2)), 1)
    rate_padded = padded[-1]
    smoothed = diffuse(padded[:-1], rate_padded, row_start, total_rows)
    padded_again = padded_2(smoothed, (("ty", 1), ("tx", 2)), 1)
    smoothed = diffuse(padded_again, rate_padded, row_start, total_rows)
    scaled = (cell_area[None] * smoothed).astype(jnp.bfloat16)
    blocks = (
        scaled.reshape(NVAR, BR, BH, BCOL, BW)
        .transpose(1, 3, 0, 2, 4)
        .reshape(BR * BCOL, NVAR, BH * BW)
    )
    chosen = blocks[pair_block]
    partials = jnp.einsum("pvc,pcd->pvd", chosen, weight_blocks, preferred_element_type=jnp.float32)
    owners = pair_owner[:, 0]
    rows_ty = lax.axis_size("ty")
    cols_tx = lax.axis_size("tx")
    device_count = rows_ty * cols_tx
    target_rows = owners * TBD + pair_target
    all_rows = jax.ops.segment_sum(partials, target_rows, num_segments=device_count * TBD)
    summed = lax.psum_scatter(all_rows, ("ty", "tx"), scatter_dimension=0, tiled=True)
    return summed / target_area[:, None, :]


def solution(mesh):
    return jax.shard_map(
        on_device,
        mesh=mesh,
        in_specs=(
            P(None, "ty", "tx"),
            P("ty", "tx"),
            P("ty", "tx"),
            P(("ty", "tx")),
            P(("ty", "tx"), None),
            P(("ty", "tx")),
            P(("ty", "tx"), None, None),
            P(("ty", "tx"), None),
        ),
        out_specs=P(("ty", "tx"), None, None),
        check_vma=False,
    )
```

profile of v0, /device:TPU:0, one launch (start us, length us, event | category | flops | bytes accessed | tf_op | source)
XLA Modules:
  0.0 768.8 jit_solution(5072553455892769984)
XLA Ops:
  6.5 1.0 pad_maximum_fusion.27
  7.5 2.6 collective-permute-start.1
  11.5 2.9 collective-permute-done
  14.4 1.3 pad_maximum_fusion
  15.9 6.3 collective-permute-start.3
  22.2 7.2 collective-permute-done.3
  29.4 5.5 collective-permute-done.2
  34.9 1.0 fusion.26
  36.2 3.3 fusion.16
  39.5 2.9 collective-permute-start.5
  42.4 1.4 collective-permute-done.5
  43.7 2.9 collective-permute-done.4
  47.5 1.5 collective-permute-start.7
  49.0 6.6 collective-permute-done.6
  55.6 3.6 collective-permute-done.7
  60.0 2.1 reshape.24
  62.1 2.5 copy.11
  64.6 4.0 reshape.25
  68.6 0.8 gather_fusion
  69.4 4.7 fusion.38
  74.1 3.5 broadcast_in_dim.50
  77.6 25.0 %scatter_fusion = f32[2048,8,128]{2,1,0:T(8,128)} fusion(f32[2048,8,128]{2,1,0:T(8,128)} %broadcast_in_dim.50, s32[256]{0:T(256)S(1)} %add.69, f32[256,8,128]{2,1,0:T(8,128)S(1)} %fusion.38), kind=kCustom, calls=%fused_computation.1 | custom fusion | flops 262144 | bytes 3146752 | tf_op jit(solution)/shard_map/scatter-add | solution.py:78
  102.6 657.8 %reduce-scatter.2.cloned.1.call-done = f32[16,8,128]{2,1,0:T(8,128)} async-done(((f32[2048,8,128]{2,1,0:T(8,128)}), f32[16,8,128]{2,1,0:T(8,128)}) %reduce-scatter.2.cloned.1.call-update) | async-done | bytes 65552 | tf_op jit(solution)/shard_map/reduce_scatter | solution.py:79
  760.5 1.5 broadcast_divide_fusion
  (26 shorter events, 3.5 us)
Async XLA Ops:
  6.5 35.8 %copy-start.3 = (s32[256,1]{0,1:T(1,128)S(1)}, s32[256,1]{0,1:T(1,128)}, u32[]{:S(2)}) copy-start(s32[256,1]{0,1:T(1,128)} %param.12) | copy-start | bytes 3076
  6.5 42.5 %copy-start.2 = (s32[256]{0:T(256)S(1)}, s32[256]{0:T(256)}, u32[]{:S(2)}) copy-start(s32[256]{0:T(256)} %param.13) | copy-start | bytes 3076
  6.5 52.7 %copy-start = (f32[96,256]{1,0:T(8,128)S(1)}, f32[96,256]{1,0:T(8,128)}, u32[]{:S(2)}) copy-start(f32[96,256]{1,0:T(8,128)} %param.10) | copy-start | bytes 294916
  6.5 753.9 %reduce-scatter.2.cloned.1.call-start = ((), (), s32[]{:S(2)}) async-start(), calls=%async_computation.1 | async-start | bytes 8454144 | tf_op jit(solution)/shard_map/reduce_scatter | solution.py:79
  7.5 4.0 collective-permute-start.1
  10.1 4.3 collective-permute-start
  15.9 13.6 %collective-permute-start.3 = (f32[9,98,1]{2,1,0:T(8,128)S(1)}, f32[9,98,1]{2,1,0:T(8,128)S(1)}, u32[]{:S(2)}, u32[]{:S(2)}) collective-permute-start(f32[9,98,1]{2,1,0:T(8,128)S(1)} %get-tuple-element.5), channel_id=1, source_target_pairs={{1,0},{2,1},{3,2},{4,3},{5,4},{6,5},{7,6},{8,7},{9,8},{10,9},{11,1... | collective-permute-start | bytes 10592 | tf_op jit(solution)/shard_map/ppermute | solution.py:22
  22.2 12.8 %collective-permute-start.2 = (f32[9,98,1]{2,1,0:T(8,128)S(1)}, f32[9,98,1]{2,1,0:T(8,128)S(1)}, u32[]{:S(2)}, u32[]{:S(2)}) collective-permute-start(f32[9,98,1]{2,1,0:T(8,128)S(1)} %get-tuple-element.6), channel_id=1, source_target_pairs={{0,1},{1,2},{2,3},{3,4},{4,5},{5,6},{6,7},{7,8},{8,9},{9,10},{10,1... | collective-permute-start | bytes 10592 | tf_op jit(solution)/shard_map/ppermute | solution.py:21
  39.5 4.2 collective-permute-start.5
  42.4 4.3 collective-permute-start.4
  46.9 8.7 %collective-permute-start.6 = (f32[8,98,1]{2,1,0:T(8,128)S(1)}, f32[8,98,1]{2,1,0:T(8,128)S(1)}, u32[]{:S(2)}, u32[]{:S(2)}) collective-permute-start(f32[8,98,1]{2,1,0:T(8,128)S(1)} %get-tuple-element.9), channel_id=1, source_target_pairs={{1,0},{2,1},{3,2},{4,3},{5,4},{6,5},{7,6},{8,7},{9,8},{10,9},{11,1... | collective-permute-start | bytes 9416 | tf_op jit(solution)/shard_map/ppermute | solution.py:22
  47.5 11.7 %collective-permute-start.7 = (f32[8,98,1]{2,1,0:T(8,128)S(1)}, f32[8,98,1]{2,1,0:T(8,128)S(1)}, u32[]{:S(2)}, u32[]{:S(2)}) collective-permute-start(f32[8,98,1]{2,1,0:T(8,128)S(1)} %get-tuple-element.10), channel_id=1, source_target_pairs={{0,1},{1,2},{2,3},{3,4},{4,5},{5,6},{6,7},{7,8},{8,9},{9,10},{10,1... | collective-permute-start | bytes 9416 | tf_op jit(solution)/shard_map/ppermute | solution.py:21
  74.1 686.4 %copy-start.1 = (f32[16,128]{1,0:T(8,128)S(1)}, f32[16,128]{1,0:T(8,128)}, u32[]{:S(2)}) copy-start(f32[16,128]{1,0:T(8,128)} %param.15) | copy-start | bytes 24580
Sparse Core Ops, SparseCore 0:
  102.7 657.6 reduce-scatter.1
where the time goes:
time: 770 us; the launch traced here: 769 us
  waiting for transfers between devices  689 us (89%)
  other arithmetic  34.8 us (5%)
  starting transfers between devices  13.8 us (2%)
  between operations  13.5 us (2%)
  local copies, waits for them, and re-layouts  13.3 us (2%)
    reduce_scatter x1, waiting for transfers between devices, on_device(): lax.psum_scatter(all_rows, ('ty', 'tx'), scatter_dimension=0, tiled=True)  658 us
    scatter-add x1, other arithmetic, on_device(): jax.ops.segment_sum(partials, target_rows, num_segments=device_count * TBD)  25 us
    ppermute x4, waiting for transfers between devices, padded_2(): after = lax.ppermute(initial, axis, down)  15.9 us
  transfers between devices with their start and end apart: 9, of which 9 were waited for; matrix products, arithmetic and copies ran while one was open for 0% of the time, Pallas kernels for 0%

commit v1 on v0

--- a/solution.py
+++ b/solution.py
@@ -1,6 +1,10 @@
+import functools
+
 import jax
 import jax.numpy as jnp
 from jax import lax
+from jax.experimental import pallas as pl
+from jax.experimental.pallas import tpu as pltpu
 from jax.sharding import PartitionSpec as P
 
 NVAR = 8
@@ -9,6 +13,9 @@
 BR = 12
 BCOL = 16
 TBD = 16
+CAP = 4
+MESH = pl.DeviceIdType.MESH
+STEP, BACK = 51, 123
 
 
 def padded_2(shard, sides, width):
@@ -43,7 +50,108 @@
     )
 
 
+def barrier(ny, nx, second):
+    ty, tx = lax.axis_index("ty"), lax.axis_index("tx")
+    first = pltpu.get_barrier_semaphore()
+    for d in range(1, nx):
+        pl.semaphore_signal(first, inc=1, device_id=(ty, lax.rem(tx + d, nx)), device_id_type=MESH)
+    for d in range(1, ny):
+        pl.semaphore_signal(first, inc=1, device_id=(lax.rem(ty + d, ny), tx), device_id_type=MESH)
+    pl.semaphore_wait(first, nx - 1 + ny - 1)
+    for d in range(1, ny):
+        pl.semaphore_signal(second, inc=1, device_id=(lax.rem(ty + d, ny), tx), device_id_type=MESH)
+    pl.semaphore_wait(second, ny - 1)
+
+
+def exchange_kernel(
+    ny, nx, send_ref, meta_ref, area_ref, out_ref,
+    got, meta_got, meta_smem, send_sem, recv_sem, meta_send_sem, meta_recv_sem, local_sem, ready,
+):
+    n = ny * nx
+    me = lax.axis_index("ty") * nx + lax.axis_index("tx")
+    barrier(ny, nx, ready)
+
+    def to(d):
+        peer = lax.rem(me + lax.rem(d * STEP, n), n)
+        return (peer // nx, lax.rem(peer, nx))
+
+    def meta_copy(d):
+        return pltpu.make_async_remote_copy(
+            src_ref=meta_ref.at[d], dst_ref=meta_got.at[d], send_sem=meta_send_sem.at[d],
+            recv_sem=meta_recv_sem.at[d], device_id=to(d), device_id_type=MESH)
+
+    def data_copy(d):
+        return pltpu.make_async_remote_copy(
+            src_ref=send_ref.at[d], dst_ref=got.at[d], send_sem=send_sem.at[d],
+            recv_sem=recv_sem.at[d], device_id=to(d), device_id_type=MESH)
+
+    def start(copy):
+        def body(d, carry):
+            copy(d).start()
+            return carry
+        lax.fori_loop(1, n, body, 0)
+
+    def finish(copy):
+        def body(d, carry):
+            copy(d).wait()
+            return carry
+        lax.fori_loop(1, n, body, 0)
+
+    start(meta_copy)
+    start(data_copy)
+    meta_got[0] = meta_ref[0]
+    got[0] = send_ref[0]
+    finish(meta_copy)
+    table = pltpu.make_async_copy(meta_got, meta_smem, local_sem)
+    table.start()
+    table.wait()
+
+    def add(d, sums):
+        sums = list(sums)
+        for k in range(CAP):
+            tile = got[d, k]
+            t = meta_smem[d, 0, k]
+            for j in range(TBD):
+                sums[j] = sums[j] + jnp.where(t == j, tile, 0.0)
+        return tuple(sums)
+
+    def body(d, sums):
+        data_copy(d).wait()
+        return add(d, sums)
+
+    zero = jnp.zeros((NVAR, BH * BW), jnp.float32)
+    sums = add(0, (zero,) * TBD)
+    sums = lax.fori_loop(1, n, body, sums)
+    for j in range(TBD):
+        out_ref[j] = sums[j] / area_ref[pl.ds(j, 1), :]
+
+
+def exchange(ny, nx, send, meta, area):
+    n = ny * nx
+    vmem = pl.BlockSpec(memory_space=pltpu.VMEM)
+    return pl.pallas_call(
+        functools.partial(exchange_kernel, ny, nx),
+        out_shape=jax.ShapeDtypeStruct((TBD, NVAR, BH * BW), jnp.float32),
+        in_specs=[vmem, vmem, vmem],
+        out_specs=vmem,
+        scratch_shapes=[
+            pltpu.VMEM((n, CAP, NVAR, BH * BW), jnp.float32),
+            pltpu.VMEM((n, 1, 128), jnp.int32),
+            pltpu.SMEM((n, 1, 128), jnp.int32),
+            pltpu.SemaphoreType.DMA((n,)),
+            pltpu.SemaphoreType.DMA((n,)),
+            pltpu.SemaphoreType.DMA((n,)),
+            pltpu.SemaphoreType.DMA((n,)),
+            pltpu.SemaphoreType.DMA,
+            pltpu.SemaphoreType.REGULAR,
+        ],
+        compiler_params=pltpu.CompilerParams(collective_id=0, has_side_effects=True),
+        name="exchange",
+    )(send, meta, area)
+
+
 def on_device(
+    ny, nx,
     source_fields,
     diffusivity,
     cell_area,
@@ -53,8 +161,9 @@
     weight_blocks,
     target_area,
 ):
+    n = ny * nx
     row_count = source_fields.shape[1]
-    total_rows = row_count * lax.axis_size("ty")
+    total_rows = row_count * ny
     row_start = lax.axis_index("ty") * row_count
     stacked = jnp.concatenate([source_fields, diffusivity[None]], axis=0)
     padded = padded_2(stacked, (("ty", 1), ("tx", 2)), 1)
@@ -71,18 +180,24 @@
     chosen = blocks[pair_block]
     partials = jnp.einsum("pvc,pcd->pvd", chosen, weight_blocks, preferred_element_type=jnp.float32)
     owners = pair_owner[:, 0]
-    rows_ty = lax.axis_size("ty")
-    cols_tx = lax.axis_size("tx")
-    device_count = rows_ty * cols_tx
-    target_rows = owners * TBD + pair_target
-    all_rows = jax.ops.segment_sum(partials, target_rows, num_segments=device_count * TBD)
-    summed = lax.psum_scatter(all_rows, ("ty", "tx"), scatter_dimension=0, tiled=True)
-    return summed / target_area[:, None, :]
+    me = lax.axis_index("ty") * nx + lax.axis_index("tx")
+    key = lax.rem(lax.rem(owners - me + n, n) * BACK, n)
+    count = owners.shape[0]
+    index = lax.iota(jnp.int32, count)
+    same = (key[:, None] == key[None, :]) & (index[:, None] > index[None, :])
+    rank = jnp.sum(same, axis=1)
+    place = key * CAP + rank
+    here = place[None, :] == lax.iota(jnp.int32, n * CAP)[:, None]
+    source = jnp.sum(jnp.where(here, index[None, :], 0), axis=1)
+    goal = jnp.sum(jnp.where(here, pair_target[None, :] + 1, 0), axis=1) - 1
+    send = partials[source].reshape(n, CAP, NVAR, BH * BW)
+    meta = jnp.pad(goal.reshape(n, 1, CAP), ((0, 0), (0, 0), (0, 128 - CAP)))
+    return exchange(ny, nx, send, meta, target_area)
 
 
 def solution(mesh):
     return jax.shard_map(
-        on_device,
+        functools.partial(on_device, mesh.shape["ty"], mesh.shape["tx"]),
         mesh=mesh,
         in_specs=(
             P(None, "ty", "tx"),

time: 770 us -> 112 us (0.15)
  the two profiles are of different devices: /device:TPU:0 before, /device:TPU:1 now
where the time goes in v1:
time: 112 us
  Pallas kernels  41.4 us (37%)
  waiting for transfers between devices  27.2 us (24%)
  starting transfers between devices  16.7 us (15%)
  local copies, waits for them, and re-layouts  14.8 us (13%)
  other arithmetic  6.69 us (6%)
  matrix products  4.66 us (4%)
    pallas_call x1, Pallas kernels, exchange(): pl.pallas_call(functools.partial(exchange_kernel, ny, nx), out_shape=jax....  41.4 us
    ppermute x4, waiting for transfers between devices, padded_2(): before = lax.ppermute(last, axis, up)  16 us
    ppermute x4, waiting for transfers between devices, padded_2(): after = lax.ppermute(initial, axis, down)  11.1 us
    ppermute x4, starting transfers between devices, padded_2(): after = lax.ppermute(initial, axis, down)  9.32 us
    ppermute x4, starting transfers between devices, padded_2(): before = lax.ppermute(last, axis, up)  7.4 us
    dot_general x1, matrix products, on_device(): jnp.einsum('pvc,pcd->pvd', chosen, weight_blocks, preferred_element_type=...  4.66 us
    reshape x2, local copies, waits for them, and re-layouts, on_device(): scaled.reshape(NVAR, BR, BH, BCOL, BW).transpose(1, 3, 0, 2, 4)  4.62 us
    reshape x1, local copies, waits for them, and re-layouts, on_device(): blocks = scaled.reshape(NVAR, BR, BH, BCOL, BW).transpose(1, 3, 0, 2, 4)....  3.98 us
  transfers between devices with their start and end apart: 8, of which 6 were waited for; matrix products, arithmetic and copies ran while one was open for 3% of the time, Pallas kernels for 0%

profile of v1, /device:TPU:1, one launch (start us, length us, event | category | flops | bytes accessed | tf_op | source)
XLA Modules:
  0.0 111.6 jit_solution(6502369696180792)
XLA Ops:
  0.0 1.0 pad_maximum_fusion.27
  1.0 2.7 %collective-permute-start = (f32[9,1,256]{2,1,0:T(1,128)S(1)}, f32[9,1,256]{2,1,0:T(1,128)S(1)}, u32[]{:S(2)}, u32[]{:S(2)}) collective-permute-start(f32[9,1,256]{2,1,0:T(1,128)S(1)} %get-tuple-element.12), channel_id=1, source_target_pairs={{0,16},{16,32},{32,48},{48,64},{64,80},{80,96},{96,112},{112,0},{1... | collective-permute-start | bytes 27656 | tf_op jit(solution)/shard_map/ppermute | solution.py:28
  3.7 0.7 compare_select_fusion.1
  4.6 0.7 multiply_add_fusion
  6.8 1.3 %pad_maximum_fusion = f32[9,98,256]{2,1,0:T(8,128)S(1)} fusion(f32[9,1,256]{2,1,0:T(1,128)S(1)} %collective-permute-done.1, f32[1,96,256]{2,1,0:T(8,128)} %bitcast.19, f32[8,96,256]{2,1,0:T(8,128)} %param.8, f32[9,1,256]{2,1,0:T(1,128)S(1)} %collective-permute-done), kind=kLoop, calls=%fused_computation.3 | loop fusion | flops 677376 | bytes 1806336 | tf_op jit(solution)/shard_map/concatenate | solution.py:30
  8.3 1.7 %collective-permute-start.2 = (f32[9,98,1]{2,1,0:T(8,128)S(1)}, f32[9,98,1]{2,1,0:T(8,128)S(1)}, u32[]{:S(2)}, u32[]{:S(2)}) collective-permute-start(f32[9,98,1]{2,1,0:T(8,128)S(1)} %get-tuple-element.10), channel_id=1, source_target_pairs={{0,1},{1,2},{2,3},{3,4},{4,5},{5,6},{6,7},{7,8},{8,9},{9,10},{10,1... | collective-permute-start | bytes 10592 | tf_op jit(solution)/shard_map/ppermute | solution.py:28
  10.0 4.4 %collective-permute-start.3 = (f32[9,98,1]{2,1,0:T(8,128)S(1)}, f32[9,98,1]{2,1,0:T(8,128)S(1)}, u32[]{:S(2)}, u32[]{:S(2)}) collective-permute-start(f32[9,98,1]{2,1,0:T(8,128)S(1)} %get-tuple-element.9), channel_id=1, source_target_pairs={{1,0},{2,1},{3,2},{4,3},{5,4},{6,5},{7,6},{8,7},{9,8},{10,9},{11,1... | collective-permute-start | bytes 10592 | tf_op jit(solution)/shard_map/ppermute | solution.py:29
  14.4 10.0 %collective-permute-done.2 = f32[9,98,1]{2,1,0:T(8,128)S(1)} collective-permute-done((f32[9,98,1]{2,1,0:T(8,128)S(1)}, f32[9,98,1]{2,1,0:T(8,128)S(1)}, u32[]{:S(2)}, u32[]{:S(2)}) %collective-permute-start.2) | collective-permute-done | bytes 3560 | tf_op jit(solution)/shard_map/ppermute | solution.py:28
  24.7 0.7 fusion.16
  25.5 3.0 %collective-permute-start.4 = (f32[8,1,256]{2,1,0:T(1,128)S(1)}, f32[8,1,256]{2,1,0:T(1,128)S(1)}, u32[]{:S(2)}, u32[]{:S(2)}) collective-permute-start(f32[8,1,256]{2,1,0:T(1,128)S(1)} %get-tuple-element.16), channel_id=1, source_target_pairs={{0,16},{16,32},{32,48},{48,64},{64,80},{80,96},{96,112},{112,0},{1... | collective-permute-start | bytes 24584 | tf_op jit(solution)/shard_map/ppermute | solution.py:28
  28.5 0.8 collective-permute-done.4
  29.3 2.3 %collective-permute-done.5 = f32[8,1,256]{2,1,0:T(1,128)S(1)} collective-permute-done((f32[8,1,256]{2,1,0:T(1,128)S(1)}, f32[8,1,256]{2,1,0:T(1,128)S(1)}, u32[]{:S(2)}, u32[]{:S(2)}) %collective-permute-start.5) | collective-permute-done | bytes 8224 | tf_op jit(solution)/shard_map/ppermute | solution.py:29
  31.9 4.9 %collective-permute-start.6 = (f32[8,98,1]{2,1,0:T(8,128)S(1)}, f32[8,98,1]{2,1,0:T(8,128)S(1)}, u32[]{:S(2)}, u32[]{:S(2)}) collective-permute-start(f32[8,98,1]{2,1,0:T(8,128)S(1)} %get-tuple-element.13), channel_id=1, source_target_pairs={{1,0},{2,1},{3,2},{4,3},{5,4},{6,5},{7,6},{8,7},{9,8},{10,9},{11,1... | collective-permute-start | bytes 9416 | tf_op jit(solution)/shard_map/ppermute | solution.py:29
  37.6 8.3 %collective-permute-done.6 = f32[8,98,1]{2,1,0:T(8,128)S(1)} collective-permute-done((f32[8,98,1]{2,1,0:T(8,128)S(1)}, f32[8,98,1]{2,1,0:T(8,128)S(1)}, u32[]{:S(2)}, u32[]{:S(2)}) %collective-permute-start.6) | collective-permute-done | bytes 3168 | tf_op jit(solution)/shard_map/ppermute | solution.py:29
  45.9 5.2 %collective-permute-done.7 = f32[8,98,1]{2,1,0:T(8,128)S(1)} collective-permute-done((f32[8,98,1]{2,1,0:T(8,128)S(1)}, f32[8,98,1]{2,1,0:T(8,128)S(1)}, u32[]{:S(2)}, u32[]{:S(2)}) %collective-permute-start.7) | collective-permute-done | bytes 3168 | tf_op jit(solution)/shard_map/ppermute | solution.py:28
  51.1 0.7 fusion.4
  51.9 2.1 %reshape.82 = bf16[8,12,8,16,16]{4,3,2,1,0:T(8,128)(2,1)S(1)} reshape(bf16[8,96,256]{2,1,0:T(8,128)(2,1)S(1)} %fusion.4) | data formatting | bytes 786432 | tf_op jit(solution)/shard_map/reshape | solution.py:176
  54.0 2.5 %copy.14 = bf16[8,12,8,16,16]{4,2,0,3,1:T(8,128)(2,1)} copy(bf16[8,12,8,16,16]{4,3,2,1,0:T(8,128)(2,1)S(1)} %reshape.82) | data formatting | bytes 786432 | tf_op jit(solution)/shard_map/reshape | solution.py:176
  56.5 4.0 %reshape.83 = bf16[192,8,128]{2,1,0:T(8,128)(2,1)S(1)} reshape(bf16[12,16,8,8,16]{4,3,2,1,0:T(8,128)(2,1)} %bitcast.16) | data formatting | bytes 786432 | tf_op jit(solution)/shard_map/reshape | solution.py:178
  60.5 0.8 gather_fusion
  61.3 4.7 %fusion.45 = f32[256,8,128]{2,1,0:T(8,128)S(1)} fusion(bf16[256,8,128]{2,1,0:T(8,128)(2,1)S(1)} %gather_fusion, bf16[256,128,128]{2,1,0:T(8,128)(2,1)} %param.14), kind=kOutput, calls=%fused_computation.103 | convolution fusion | flops 67108864 | bytes 9961472 | tf_op jit(solution)/shard_map/pvc,pcd->pvd/dot_general | solution.py:181
  66.0 2.7 %gather_fusion.1 = f32[512,8,128]{2,1,0:T(8,128)} fusion(f32[256,8,128]{2,1,0:T(8,128)S(1)} %fusion.45, s32[1024]{0:T(1024)S(1)} %pad_clamp_fusion), kind=kCustom, calls=%fused_computation.1 | custom fusion | bytes 4196352 | tf_op jit(solution)/shard_map/gather | solution.py:193
  68.7 41.4 %exchange.1 = f32[16,8,128]{2,1,0:T(8,128)} custom-call(f32[128,4,8,128]{3,2,1,0:T(8,128)} %bitcast.17, s32[128,1,128]{2,1,0:T(1,128)} %pad.4.meta_ref, f32[16,128]{1,0:T(8,128)} %area_ref.1), custom_call_target="tpu_custom_call" | custom-call | tf_op jit(solution)/shard_map/exchange/pallas_call | solution.py:132
  110.1 1.5 %copy.16 = f32[16,8,128]{2,1,0:T(8,128)} copy(f32[16,8,128]{2,1,0:T(8,128)} %exchange.1) | data formatting | bytes 131072
  (29 shorter events, 3.3 us)
Async XLA Ops:
  0.0 24.4 %copy-start.1 = (f32[96,256]{1,0:T(8,128)S(1)}, f32[96,256]{1,0:T(8,128)}, u32[]{:S(2)}) copy-start(f32[96,256]{1,0:T(8,128)} %param.9) | copy-start | bytes 294916
  0.0 24.4 %copy-start = (f32[8,96,256]{2,1,0:T(8,128)S(1)}, f32[8,96,256]{2,1,0:T(8,128)}, u32[]{:S(2)}) copy-start(f32[8,96,256]{2,1,0:T(8,128)} %param.8) | copy-start | bytes 2359300
  1.0 5.2 %collective-permute-start = (f32[9,1,256]{2,1,0:T(1,128)S(1)}, f32[9,1,256]{2,1,0:T(1,128)S(1)}, u32[]{:S(2)}, u32[]{:S(2)}) collective-permute-start(f32[9,1,256]{2,1,0:T(1,128)S(1)} %get-tuple-element.12), channel_id=1, source_target_pairs={{0,16},{16,32},{32,48},{48,64},{64,80},{80,96},{96,112},{112,0},{1... | collective-permute-start | bytes 27656 | tf_op jit(solution)/shard_map/ppermute | solution.py:28
  3.7 3.1 %collective-permute-start.1 = (f32[9,1,256]{2,1,0:T(1,128)S(1)}, f32[9,1,256]{2,1,0:T(1,128)S(1)}, u32[]{:S(2)}, u32[]{:S(2)}) collective-permute-start(f32[9,1,256]{2,1,0:T(1,128)S(1)} %get-tuple-element.11), channel_id=1, source_target_pairs={{16,0},{32,16},{48,32},{64,48},{80,64},{96,80},{112,96},{0,112},{1... | collective-permute-start | bytes 27656 | tf_op jit(solution)/shard_map/ppermute | solution.py:29
  8.3 16.1 %collective-permute-start.2 = (f32[9,98,1]{2,1,0:T(8,128)S(1)}, f32[9,98,1]{2,1,0:T(8,128)S(1)}, u32[]{:S(2)}, u32[]{:S(2)}) collective-permute-start(f32[9,98,1]{2,1,0:T(8,128)S(1)} %get-tuple-element.10), channel_id=1, source_target_pairs={{0,1},{1,2},{2,3},{3,4},{4,5},{5,6},{6,7},{7,8},{8,9},{9,10},{10,1... | collective-permute-start | bytes 10592 | tf_op jit(solution)/shard_map/ppermute | solution.py:28
  10.0 14.4 %collective-permute-start.3 = (f32[9,98,1]{2,1,0:T(8,128)S(1)}, f32[9,98,1]{2,1,0:T(8,128)S(1)}, u32[]{:S(2)}, u32[]{:S(2)}) collective-permute-start(f32[9,98,1]{2,1,0:T(8,128)S(1)} %get-tuple-element.9), channel_id=1, source_target_pairs={{1,0},{2,1},{3,2},{4,3},{5,4},{6,5},{7,6},{8,7},{9,8},{10,9},{11,1... | collective-permute-start | bytes 10592 | tf_op jit(solution)/shard_map/ppermute | solution.py:29
  25.5 25.7 %copy-start.2 = (f32[96,256]{1,0:T(8,128)S(1)}, f32[96,256]{1,0:T(8,128)}, u32[]{:S(2)}) copy-start(f32[96,256]{1,0:T(8,128)} %param.10) | copy-start | bytes 294916
  25.5 3.8 %collective-permute-start.4 = (f32[8,1,256]{2,1,0:T(1,128)S(1)}, f32[8,1,256]{2,1,0:T(1,128)S(1)}, u32[]{:S(2)}, u32[]{:S(2)}) collective-permute-start(f32[8,1,256]{2,1,0:T(1,128)S(1)} %get-tuple-element.16), channel_id=1, source_target_pairs={{0,16},{16,32},{32,48},{48,64},{64,80},{80,96},{96,112},{112,0},{1... | collective-permute-start | bytes 24584 | tf_op jit(solution)/shard_map/ppermute | solution.py:28
  28.5 3.1 %collective-permute-start.5 = (f32[8,1,256]{2,1,0:T(1,128)S(1)}, f32[8,1,256]{2,1,0:T(1,128)S(1)}, u32[]{:S(2)}, u32[]{:S(2)}) collective-permute-start(f32[8,1,256]{2,1,0:T(1,128)S(1)} %get-tuple-element.15), channel_id=1, source_target_pairs={{16,0},{32,16},{48,32},{64,48},{80,64},{96,80},{112,96},{0,112},{1... | collective-permute-start | bytes 24584 | tf_op jit(solution)/shard_map/ppermute | solution.py:29
  31.9 14.0 %collective-permute-start.6 = (f32[8,98,1]{2,1,0:T(8,128)S(1)}, f32[8,98,1]{2,1,0:T(8,128)S(1)}, u32[]{:S(2)}, u32[]{:S(2)}) collective-permute-start(f32[8,98,1]{2,1,0:T(8,128)S(1)} %get-tuple-element.13), channel_id=1, source_target_pairs={{1,0},{2,1},{3,2},{4,3},{5,4},{6,5},{7,6},{8,7},{9,8},{10,9},{11,1... | collective-permute-start | bytes 9416 | tf_op jit(solution)/shard_map/ppermute | solution.py:29
  36.8 14.4 %collective-permute-start.7 = (f32[8,98,1]{2,1,0:T(8,128)S(1)}, f32[8,98,1]{2,1,0:T(8,128)S(1)}, u32[]{:S(2)}, u32[]{:S(2)}) collective-permute-start(f32[8,98,1]{2,1,0:T(8,128)S(1)} %get-tuple-element.14), channel_id=1, source_target_pairs={{0,1},{1,2},{2,3},{3,4},{4,5},{5,6},{6,7},{7,8},{8,9},{9,10},{10,1... | collective-permute-start | bytes 9416 | tf_op jit(solution)/shard_map/ppermute | solution.py:28

commit v2 on v0

v2 whole, which is shorter than its diff:
```python
import functools

import jax
import jax.numpy as jnp
from jax import lax
from jax.experimental import pallas as pl
from jax.experimental.pallas import tpu as pltpu
from jax.sharding import PartitionSpec as P

NVAR = 8
BH = 8
BW = 16
BR = 12
BCOL = 16
TBD = 16
CAP = 4
CELLS = BH * BW
MESH = pl.DeviceIdType.MESH
STEP, BACK = 51, 123
GROUP = 16
SLOTS = GROUP // CAP


def kernel(
    ny, nx,
    fields_ref, rate_ref, area_ref, block_ref, owner_ref, target_ref, weight_ref, target_area_ref,
    out_ref,
    x, y, rate, k_east, k_west, k_north, k_south, pack, from_west, from_east, s0, s1,
    blocks, weights, part, send, got, tables, tables_smem, goal, meta, meta_got, meta_smem,
    local_sem, edge_send, edge_recv, data_send, data_recv, meta_send, meta_recv, ready,
):
    n = ny * nx
    rows, cols = rate_ref.shape
    pairs = weight_ref.shape[0]
    total_rows = rows * ny
    ty, tx = lax.axis_index("ty"), lax.axis_index("tx")
    me = ty * nx + tx
    north, south = lax.rem(ty + 1, ny), lax.rem(ty + ny - 1, ny)
    east, west = lax.rem(tx + 1, nx), lax.rem(tx + nx - 1, nx)
    corners = [(north, east), (north, west), (south, east), (south, west)]

    entry = pltpu.get_barrier_semaphore()
    mates = [(ty, lax.rem(tx + d, nx)) for d in range(1, nx)]
    mates += [(lax.rem(ty + d, ny), tx) for d in range(1, ny)]
    mates += corners
    for mate in mates:
        pl.semaphore_signal(entry, inc=1, device_id=mate, device_id_type=MESH)

    own = slice(8, 8 + rows)
    load_fields = pltpu.make_async_copy(fields_ref, x.at[:, own, 0:cols], local_sem.at[0])
    load_rate = pltpu.make_async_copy(rate_ref, rate.at[own, 0:cols], local_sem.at[1])
    load_weights = pltpu.make_async_copy(weight_ref, weights, local_sem.at[2])
    load_fields.start()
    load_rate.start()
    load_weights.start()
    load_fields.wait()
    load_rate.wait()

    lane = lax.broadcasted_iota(jnp.int32, (8, 128), 1)
    for i in range(rows // 8):
        band = slice(8 + 8 * i, 16 + 8 * i)
        packed = jnp.zeros((8, 128), jnp.float32)
        for v in range(NVAR + 1):
            if v < NVAR:
                first, last = x[v, band, 0:128], x[v, band, cols - 128:cols]
            else:
                first, last = rate[band, 0:128], rate[band, cols - 128:cols]
            edge = jnp.where(lane < 64, first, last)
            if v:
                edge = pltpu.roll(edge, 4 * v, 1)
            here = (lane >= 4 * v - 2) & (lane < 4 * v + 2)
            if v == 0:
                here = here | (lane >= 126)
            packed = jnp.where(here, edge, packed)
        pack[8 * i:8 * i + 8, :] = packed

    pl.semaphore_wait(entry, len(mates))

    def edge_copy(i, src, dst, device):
        return pltpu.make_async_remote_copy(
            src_ref=src, dst_ref=dst, send_sem=edge_send.at[i], recv_sem=edge_recv.at[i],
            device_id=device, device_id_type=MESH)

    low, high = slice(0, 8), slice(8 + rows, 16 + rows)
    top, bottom = slice(rows - 8, rows), slice(0, 8)
    edges = [
        (pack, from_west.at[own], (ty, east)),
        (pack, from_east.at[own], (ty, west)),
        (pack.at[top], from_west.at[low], corners[0]),
        (pack.at[top], from_east.at[low], corners[1]),
        (pack.at[bottom], from_west.at[high], corners[2]),
        (pack.at[bottom], from_east.at[high], corners[3]),
        (rate_ref.at[top], rate.at[low, 0:cols], (north, tx)),
        (rate_ref.at[bottom], rate.at[high, 0:cols], (south, tx)),
        (fields_ref.at[:, top], x.at[:, low, 0:cols], (north, tx)),
        (fields_ref.at[:, bottom], x.at[:, high, 0:cols], (south, tx)),
    ]
    edges = [edge_copy(i, *edge) for i, edge in enumerate(edges)]
    for edge in edges:
        edge.start()
    for d in range(1, ny):
        pl.semaphore_signal(ready, inc=1, device_id=(lax.rem(ty + d, ny), tx), device_id_type=MESH)

    p_lane = lax.broadcasted_iota(jnp.int32, (1, pairs), 1)
    p_row = lax.broadcasted_iota(jnp.int32, (pairs, 1), 0)
    key_row = jnp.bitwise_and((owner_ref[...] - me + n) * BACK, n - 1)
    joint_row = p_lane * 4096 + block_ref[...] * TBD + target_ref[...]
    goal_row = target_ref[...] + 1
    eye = lax.broadcasted_iota(jnp.int32, (pairs, pairs), 0) == lax.broadcasted_iota(jnp.int32, (pairs, pairs), 1)

    def along(axis, mask, value):
        return jnp.sum(jnp.where(mask, value, 0), axis=axis, keepdims=True, dtype=jnp.int32)

    unique_row = key_row * pairs + p_lane
    key_col = along(1, eye, key_row)
    joint_col = along(1, eye, joint_row)
    unique_col = key_col * pairs + p_row
    place_row = along(0, unique_col < unique_row, 1)
    place_col = along(1, unique_row < unique_col, 1)
    joint = along(0, place_col == p_lane, joint_col)
    tables[0:1, :] = jnp.clip(lax.shift_right_logical(joint, 12), 0, pairs - 1)
    tables[1:2, :] = jnp.clip(jnp.bitwise_and(lax.shift_right_logical(joint, 4), 255), 0, blocks.shape[0] - 1)
    tables[2:3, :] = along(0, key_col < p_lane, 1)
    table_copy = pltpu.make_async_copy(tables, tables_smem, local_sem.at[3])
    table_copy.start()

    d_col = lax.broadcasted_iota(jnp.int32, (n, 1), 0)
    rank = jnp.where(key_row == d_col, place_row - along(1, key_row < d_col, 1), -1)
    d_lane = lax.broadcasted_iota(jnp.int32, (n, 128), 1)
    goals = jnp.zeros((n, 128), jnp.int32)
    for k in range(CAP):
        goals = jnp.where(d_lane == k, along(1, rank == k, goal_row), goals)
    goal[...] = goals - 1
    for d in range(n):
        meta[d] = goal[d:d + 1, :]

    def peer(d):
        p = lax.rem(me + lax.rem(d * STEP, n), n)
        return (p // nx, lax.rem(p, nx))

    def meta_copy(d):
        return pltpu.make_async_remote_copy(
            src_ref=meta.at[d], dst_ref=meta_got.at[d], send_sem=meta_send.at[d],
            recv_sem=meta_recv.at[d], device_id=peer(d), device_id_type=MESH)

    def data_copy(d):
        return pltpu.make_async_remote_copy(
            src_ref=send.at[d], dst_ref=got.at[d], send_sem=data_send.at[d],
            recv_sem=data_recv.at[d], device_id=peer(d), device_id_type=MESH)

    def every(start, stop, action):
        def body(d, carry):
            action(d)
            return carry
        lax.fori_loop(start, stop, body, 0)

    pl.semaphore_wait(ready, ny - 1)
    meta_got[0] = meta[0]
    every(1, n, lambda d: meta_copy(d).start())

    for edge in edges:
        edge.wait()

    for i in range((rows + 16) // 8):
        band = slice(8 * i, 8 * i + 8)
        both = jnp.where(jnp.bitwise_and(lane, 3) < 2, from_east[band, :], from_west[band, :])
        for v in range(NVAR):
            x[v, band, cols:cols + 128] = pltpu.roll(both, (128 - 4 * v) % 128, 1) if v else both
        rate[band, cols:cols + 128] = pltpu.roll(both, 128 - 4 * NVAR, 1)

    wide = cols + 128
    bands = (rows + 8) // 8
    sub = lax.broadcasted_iota(jnp.int32, (8, wide), 0)
    for i in range(bands):
        a = 7 + 8 * i
        centre = rate[a:a + 8, :]
        g = sub + (ty * rows + 8 * i - 1)
        band = slice(8 * i, 8 * i + 8)
        k_east[band, :] = 0.5 * (centre + pltpu.roll(centre, wide - 1, 1))
        k_west[band, :] = 0.5 * (centre + pltpu.roll(centre, 1, 1))
        k_north[band, :] = jnp.where(g < total_rows - 1, 0.5 * (centre + rate[a + 1:a + 9, :]), 0.0)
        k_south[band, :] = jnp.where(g > 0, 0.5 * (centre + rate[a - 1:a + 7, :]), 0.0)

    def smooth(v, carry):
        for i in range(bands):
            a = 7 + 8 * i
            band = slice(8 * i, 8 * i + 8)
            c = x[v, a:a + 8, :]
            y[v, band, :] = (
                c
                + k_east[band, :] * (pltpu.roll(c, wide - 1, 1) - c)
                + k_west[band, :] * (pltpu.roll(c, 1, 1) - c)
                + k_north[band, :] * (x[v, a + 1:a + 9, :] - c)
                + k_south[band, :] * (x[v, a - 1:a + 7, :] - c)
            )
        for i in range(rows // 8):
            a = 8 * i + 1
            band = slice(a, a + 8)
            c = y[v, band, :]
            e = pltpu.roll(c, wide - 1, 1)[:, :cols]
            w = pltpu.roll(c, 1, 1)[:, :cols]
            c = c[:, :cols]
            z = (
                c
                + k_east[band, 0:cols] * (e - c)
                + k_west[band, 0:cols] * (w - c)
                + k_north[band, 0:cols] * (y[v, a + 1:a + 9, 0:cols] - c)
                + k_south[band, 0:cols] * (y[v, a - 1:a + 7, 0:cols] - c)
            )
            z = area_ref[8 * i:8 * i + 8, :] * z
            r = pl.multiple_of(v * rows + 8 * i, 8)
            s0[pl.ds(r, 8), :] = z[:, 0:128]
            s1[pl.ds(r, 8), :] = z[:, 128:256]
        return carry

    lax.fori_loop(0, NVAR, smooth, 0)

    def form(r, carry):
        for t, s in enumerate((s0, s1)):
            tiles = [s[pl.ds(r * BH + j, NVAR, stride=rows), :] for j in range(BH)]
            for bit in (1, 2, 4):
                mask = jnp.bitwise_and(lane, 16 * bit) == 0
                for j in range(BH):
                    if j & bit:
                        continue
                    lo, hi = tiles[j], tiles[j + bit]
                    tiles[j] = jnp.where(mask, lo, pltpu.roll(hi, 16 * bit, 1))
                    tiles[j + bit] = jnp.where(mask, pltpu.roll(lo, 128 - 16 * bit, 1), hi)
            for j in range(BH):
                blocks[r * BCOL + t * BH + j] = tiles[j]
        return carry

    lax.fori_loop(0, rows // BH, form, 0)

    table_copy.wait()
    load_weights.wait()

    def multiply(q):
        for u in range(GROUP):
            i = q * GROUP + u
            a = blocks[tables_smem[1, i]].astype(jnp.bfloat16)
            part[i] = jnp.dot(a, weights[tables_smem[0, i]], preferred_element_type=jnp.float32)

    def fill(q):
        for u in range(SLOTS):
            d = q * SLOTS + u
            first = tables_smem[2, d]
            for k in range(CAP):
                send[d, k] = part[jnp.minimum(first + k, pairs - 1)]

    def launch(q):
        for u in range(SLOTS):
            data_copy(q * SLOTS + u).start()

    last = n // SLOTS
    groups = pairs // GROUP
    multiply(0)
    fill(0)
    multiply(1)
    for u in range(1, SLOTS):
        data_copy(u).start()
    fill(1)
    multiply(2)

    def busy(q):
        launch(q - 2)
        fill(q - 1)
        multiply(q)

    def rest(q):
        launch(q - 2)
        fill(q - 1)

    every(3, groups, busy)
    every(groups, last + 1, rest)
    launch(last - 1)

    every(1, n, lambda d: meta_copy(d).wait())
    table = pltpu.make_async_copy(meta_got, meta_smem, local_sem.at[4])
    table.start()
    table.wait()

    def add(tiles, d, sums):
        sums = list(sums)
        for k in range(CAP):
            tile = tiles[d, k]
            t = meta_smem[d, 0, k]
            for j in range(TBD):
                sums[j] = sums[j] + jnp.where(t == j, tile, 0.0)
        return tuple(sums)

    def collect(d, sums):
        data_copy(d).wait()
        return add(got, d, sums)

    zero = jnp.zeros((NVAR, CELLS), jnp.float32)
    sums = add(send, 0, (zero,) * TBD)
    sums = lax.fori_loop(1, n, collect, sums)
    for j in range(TBD):
        out_ref[j] = sums[j] / target_area_ref[j:j + 1, :]


def on_device(
    ny, nx,
    source_fields,
    diffusivity,
    cell_area,
    pair_block,
    pair_owner,
    pair_target,
    weight_blocks,
    target_area,
):
    n = ny * nx
    nvar, rows, cols = source_fields.shape
    pairs = weight_blocks.shape[0]
    vmem = pl.BlockSpec(memory_space=pltpu.VMEM)
    hbm = pl.BlockSpec(memory_space=pltpu.HBM)
    f32, i32 = jnp.float32, jnp.int32
    wide, tall = cols + 128, rows + 16
    sem = pltpu.SemaphoreType.DMA
    return pl.pallas_call(
        functools.partial(kernel, ny, nx),
        out_shape=jax.ShapeDtypeStruct((TBD, NVAR, CELLS), f32),
        in_specs=[hbm, hbm, vmem, vmem, vmem, vmem, hbm, vmem],
        out_specs=vmem,
        scratch_shapes=[
            pltpu.VMEM((nvar, tall, wide), f32),
            pltpu.VMEM((nvar, tall, wide), f32),
            pltpu.VMEM((tall, wide), f32),
            pltpu.VMEM((tall, wide), f32),
            pltpu.VMEM((tall, wide), f32),
            pltpu.VMEM((tall, wide), f32),
            pltpu.VMEM((tall, wide), f32),
            pltpu.VMEM((rows, 128), f32),
            pltpu.VMEM((tall, 128), f32),
            pltpu.VMEM((tall, 128), f32),
            pltpu.VMEM((nvar * rows, 128), f32),
            pltpu.VMEM((nvar * rows, 128), f32),
            pltpu.VMEM((rows // BH * BCOL, NVAR, CELLS), f32),
            pltpu.VMEM((pairs, CELLS, CELLS), jnp.bfloat16),
            pltpu.VMEM((pairs, NVAR, CELLS), f32),
            pltpu.VMEM((n, CAP, NVAR, CELLS), f32),
            pltpu.VMEM((n, CAP, NVAR, CELLS), f32),
            pltpu.VMEM((8, pairs), i32),
            pltpu.SMEM((8, pairs), i32),
            pltpu.VMEM((n, 128), i32),
            pltpu.VMEM((n, 1, 128), i32),
            pltpu.VMEM((n, 1, 128), i32),
            pltpu.SMEM((n, 1, 128), i32),
            sem((5,)),
            sem((10,)),
            sem((10,)),
            sem((n,)),
            sem((n,)),
            sem((n,)),
            sem((n,)),
            pltpu.SemaphoreType.REGULAR,
        ],
        compiler_params=pltpu.CompilerParams(
            collective_id=0, has_side_effects=True, vmem_limit_bytes=62 * 1024 * 1024),
        name="regrid",
    )(
        source_fields, diffusivity, cell_area, pair_block.reshape(1, pairs), pair_owner.reshape(1, pairs),
        pair_target.reshape(1, pairs), weight_blocks, target_area,
    )


def solution(mesh):
    return jax.shard_map(
        functools.partial(on_device, mesh.shape["ty"], mesh.shape["tx"]),
        mesh=mesh,
        in_specs=(
            P(None, "ty", "tx"),
            P("ty", "tx"),
            P("ty", "tx"),
            P(("ty", "tx")),
            P(("ty", "tx"), None),
            P(("ty", "tx")),
            P(("ty", "tx"), None, None),
            P(("ty", "tx"), None),
        ),
        out_specs=P(("ty", "tx"), None, None),
        check_vma=False,
    )
```

time: 770 us -> 55.3 us (0.07)
  the two profiles are of different devices: /device:TPU:0 before, /device:TPU:1 now
where the time goes in v2:
time: 55.3 us; the launch traced here: 54.6 us
  Pallas kernels  53.1 us (96%)
  local copies, waits for them, and re-layouts  1.47 us (3%)
    pallas_call x1, Pallas kernels, on_device(): pl.pallas_call(functools.partial(kernel, ny, nx), out_shape=jax.ShapeDtyp...  53.1 us
    unnamed x1, local copies, waits for them, and re-layouts  1.47 us

profile of v2, /device:TPU:1, one launch (start us, length us, event | category | flops | bytes accessed | tf_op | source)
XLA Modules:
  0.0 54.6 jit_solution(10101349846086823144)
XLA Ops:
  0.0 53.1 %regrid.1 = f32[16,8,128]{2,1,0:T(8,128)} custom-call(f32[8,96,256]{2,1,0:T(8,128)} %fields_ref.1, f32[96,256]{1,0:T(8,128)} %rate_ref.1, f32[96,256]{1,0:T(8,128)} %area_ref.1, s32[1,256]{1,0:T(1,128)} %bitcast.3, s32[1,256]{1,0:T(1,128)} %bitcast.4, s32[1,256]{1,0:T(1,128)} %bitcast.5, bf16[256,128,128]{2,1,0:T(8,128)(2,1)} %weight_ref.1, ...), custom_call_target="tpu_custom_call" | custom-call | tf_op jit(solution)/shard_map/regrid/pallas_call | solution.py:322
  53.1 1.5 %copy.10 = f32[16,8,128]{2,1,0:T(8,128)} copy(f32[16,8,128]{2,1,0:T(8,128)} %regrid.1) | data formatting | bytes 131072

commit v3 on v2

--- a/solution.py
+++ b/solution.py
@@ -19,15 +19,18 @@
 STEP, BACK = 51, 123
 GROUP = 16
 SLOTS = GROUP // CAP
+FOLD = 4
+FORM = 3
 
 
 def kernel(
     ny, nx,
     fields_ref, rate_ref, area_ref, block_ref, owner_ref, target_ref, weight_ref, target_area_ref,
     out_ref,
-    x, y, rate, k_east, k_west, k_north, k_south, pack, from_west, from_east, s0, s1,
-    blocks, weights, part, send, got, tables, tables_smem, goal, meta, meta_got, meta_smem,
-    local_sem, edge_send, edge_recv, data_send, data_recv, meta_send, meta_recv, ready,
+    x, y, rate, k_east, k_west, k_north, k_south, pack, from_west, from_east,
+    up, down, from_south, from_north, s0, s1,
+    blocks, weights, part, send, got, tables, tables_smem, goal, relay, sorted_goal, goal_got, goal_smem,
+    local_sem, edge_send, edge_recv, data_send, data_recv, goal_send, goal_recv, ready,
 ):
     n = ny * nx
     rows, cols = rate_ref.shape
@@ -57,22 +60,21 @@
     load_rate.wait()
 
     lane = lax.broadcasted_iota(jnp.int32, (8, 128), 1)
-    for i in range(rows // 8):
-        band = slice(8 + 8 * i, 16 + 8 * i)
+    for j in range(FOLD):
         packed = jnp.zeros((8, 128), jnp.float32)
-        for v in range(NVAR + 1):
-            if v < NVAR:
-                first, last = x[v, band, 0:128], x[v, band, cols - 128:cols]
-            else:
-                first, last = rate[band, 0:128], rate[band, cols - 128:cols]
-            edge = jnp.where(lane < 64, first, last)
-            if v:
-                edge = pltpu.roll(edge, 4 * v, 1)
-            here = (lane >= 4 * v - 2) & (lane < 4 * v + 2)
-            if v == 0:
-                here = here | (lane >= 126)
-            packed = jnp.where(here, edge, packed)
-        pack[8 * i:8 * i + 8, :] = packed
+        for g in range(rows // (8 * FOLD)):
+            a = 8 + 8 * (j + FOLD * g)
+            for v in range(NVAR + 1):
+                field = x.at[v] if v < NVAR else rate
+                edge = jnp.where(lane < 64, field[a:a + 8, 0:128], field[a:a + 8, cols - 128:cols])
+                at = 40 * g + 4 * v
+                edge = pltpu.roll(edge, at + 2, 1)
+                packed = jnp.where((lane >= at) & (lane < at + 4), edge, packed)
+        pack[8 * j:8 * j + 8, :] = packed
+    for v in range(NVAR + 1):
+        field = x.at[v] if v < NVAR else rate
+        up[2 * v:2 * v + 2, :] = field[6 + rows:8 + rows, 0:cols]
+        down[2 * v:2 * v + 2, :] = field[8:10, 0:cols]
 
     pl.semaphore_wait(entry, len(mates))
 
@@ -81,19 +83,17 @@
             src_ref=src, dst_ref=dst, send_sem=edge_send.at[i], recv_sem=edge_recv.at[i],
             device_id=device, device_id_type=MESH)
 
-    low, high = slice(0, 8), slice(8 + rows, 16 + rows)
-    top, bottom = slice(rows - 8, rows), slice(0, 8)
+    main, low, high = slice(8, 8 + 8 * FOLD), slice(0, 8), slice(8 + 8 * FOLD, 16 + 8 * FOLD)
+    top, bottom = slice(8 * FOLD - 8, 8 * FOLD), slice(0, 8)
     edges = [
-        (pack, from_west.at[own], (ty, east)),
-        (pack, from_east.at[own], (ty, west)),
         (pack.at[top], from_west.at[low], corners[0]),
         (pack.at[top], from_east.at[low], corners[1]),
         (pack.at[bottom], from_west.at[high], corners[2]),
         (pack.at[bottom], from_east.at[high], corners[3]),
-        (rate_ref.at[top], rate.at[low, 0:cols], (north, tx)),
-        (rate_ref.at[bottom], rate.at[high, 0:cols], (south, tx)),
-        (fields_ref.at[:, top], x.at[:, low, 0:cols], (north, tx)),
-        (fields_ref.at[:, bottom], x.at[:, high, 0:cols], (south, tx)),
+        (pack, from_west.at[main], (ty, east)),
+        (pack, from_east.at[main], (ty, west)),
+        (up, from_south, (north, tx)),
+        (down, from_north, (south, tx)),
     ]
     edges = [edge_copy(i, *edge) for i, edge in enumerate(edges)]
     for edge in edges:
@@ -124,24 +124,38 @@
     table_copy = pltpu.make_async_copy(tables, tables_smem, local_sem.at[3])
     table_copy.start()
 
-    d_col = lax.broadcasted_iota(jnp.int32, (n, 1), 0)
+    r_col = lax.broadcasted_iota(jnp.int32, (n, 1), 0)
+    owner_col = lax.rem(r_col, ny) * nx + lax.div(r_col, ny)
+    d_col = jnp.bitwise_and((owner_col - me + n) * BACK, n - 1)
     rank = jnp.where(key_row == d_col, place_row - along(1, key_row < d_col, 1), -1)
     d_lane = lax.broadcasted_iota(jnp.int32, (n, 128), 1)
     goals = jnp.zeros((n, 128), jnp.int32)
     for k in range(CAP):
         goals = jnp.where(d_lane == k, along(1, rank == k, goal_row), goals)
     goal[...] = goals - 1
-    for d in range(n):
-        meta[d] = goal[d:d + 1, :]
+
+    def rows_of(i, size):
+        return pl.ds(pl.multiple_of(i * size, 8), size)
+
+    def goal_copy(i, src, dst, device):
+        return pltpu.make_async_remote_copy(
+            src_ref=src, dst_ref=dst, send_sem=goal_send.at[i], recv_sem=goal_recv.at[i],
+            device_id=device, device_id_type=MESH)
+
+    along_tx, along_ty = [], []
+    for d in range(1, nx):
+        to = lax.rem(tx + d, nx)
+        along_tx.append(goal_copy(d, goal.at[rows_of(to, ny)], relay.at[rows_of(tx, ny)], (ty, to)))
+    for d in range(1, ny):
+        to = lax.rem(ty + d, ny)
+        along_ty.append(goal_copy(nx + d, sorted_goal.at[rows_of(to, nx)], goal_got.at[rows_of(ty, nx)], (to, tx)))
+    for copy in along_tx:
+        copy.start()
+    relay[rows_of(tx, ny), :] = goal[rows_of(tx, ny), :]
 
     def peer(d):
         p = lax.rem(me + lax.rem(d * STEP, n), n)
         return (p // nx, lax.rem(p, nx))
-
-    def meta_copy(d):
-        return pltpu.make_async_remote_copy(
-            src_ref=meta.at[d], dst_ref=meta_got.at[d], send_sem=meta_send.at[d],
-            recv_sem=meta_recv.at[d], device_id=peer(d), device_id_type=MESH)
 
     def data_copy(d):
         return pltpu.make_async_remote_copy(
@@ -154,19 +168,29 @@
             return carry
         lax.fori_loop(start, stop, body, 0)
 
-    pl.semaphore_wait(ready, ny - 1)
-    meta_got[0] = meta[0]
-    every(1, n, lambda d: meta_copy(d).start())
-
     for edge in edges:
         edge.wait()
 
-    for i in range((rows + 16) // 8):
+    both = []
+    for i in range(FOLD + 2):
         band = slice(8 * i, 8 * i + 8)
-        both = jnp.where(jnp.bitwise_and(lane, 3) < 2, from_east[band, :], from_west[band, :])
-        for v in range(NVAR):
-            x[v, band, cols:cols + 128] = pltpu.roll(both, (128 - 4 * v) % 128, 1) if v else both
-        rate[band, cols:cols + 128] = pltpu.roll(both, 128 - 4 * NVAR, 1)
+        both.append(jnp.where(jnp.bitwise_and(lane, 3) < 2, from_west[band, :], from_east[band, :]))
+    folds = rows // (8 * FOLD)
+    for i in range(-1, rows // 8 + 1):
+        if i < 0:
+            tile, g = both[0], folds - 1
+        elif i == rows // 8:
+            tile, g = both[-1], 0
+        else:
+            tile, g = both[1 + i % FOLD], i // FOLD
+        band = slice(8 + 8 * i, 16 + 8 * i)
+        for v in range(NVAR + 1):
+            field = x.at[v] if v < NVAR else rate
+            field[band, cols:cols + 128] = pltpu.roll(tile, 126 - 40 * g - 4 * v, 1)
+    for v in range(NVAR + 1):
+        field = x.at[v] if v < NVAR else rate
+        field[6:8, 0:cols] = from_south[2 * v:2 * v + 2, :]
+        field[8 + rows:10 + rows, 0:cols] = from_north[2 * v:2 * v + 2, :]
 
     wide = cols + 128
     bands = (rows + 8) // 8
@@ -215,22 +239,24 @@
 
     lax.fori_loop(0, NVAR, smooth, 0)
 
-    def form(r, carry):
-        for t, s in enumerate((s0, s1)):
-            tiles = [s[pl.ds(r * BH + j, NVAR, stride=rows), :] for j in range(BH)]
-            for bit in (1, 2, 4):
-                mask = jnp.bitwise_and(lane, 16 * bit) == 0
+    def form(q, carry):
+        group = [(q * FORM + u, t, s) for u in range(FORM) for t, s in enumerate((s0, s1))]
+        tiles = [[s[pl.ds(r * BH + j, NVAR, stride=rows), :] for j in range(BH)] for r, t, s in group]
+        for bit in (1, 2, 4):
+            mask = jnp.bitwise_and(lane, 16 * bit) == 0
+            for tile in tiles:
                 for j in range(BH):
                     if j & bit:
                         continue
-                    lo, hi = tiles[j], tiles[j + bit]
-                    tiles[j] = jnp.where(mask, lo, pltpu.roll(hi, 16 * bit, 1))
-                    tiles[j + bit] = jnp.where(mask, pltpu.roll(lo, 128 - 16 * bit, 1), hi)
+                    lo, hi = tile[j], tile[j + bit]
+                    tile[j] = jnp.where(mask, lo, pltpu.roll(hi, 16 * bit, 1))
+                    tile[j + bit] = jnp.where(mask, pltpu.roll(lo, 128 - 16 * bit, 1), hi)
+        for (r, t, s), tile in zip(group, tiles):
             for j in range(BH):
-                blocks[r * BCOL + t * BH + j] = tiles[j]
+                blocks[r * BCOL + t * BH + j] = tile[j]
         return carry
 
-    lax.fori_loop(0, rows // BH, form, 0)
+    lax.fori_loop(0, rows // BH // FORM, form, 0)
 
     table_copy.wait()
     load_weights.wait()
@@ -257,11 +283,23 @@
     multiply(0)
     fill(0)
     multiply(1)
+    pl.semaphore_wait(ready, ny - 1)
     for u in range(1, SLOTS):
         data_copy(u).start()
     fill(1)
     multiply(2)
 
+    for copy in along_tx:
+        copy.wait()
+    for i in range(ny):
+        sorted_goal[i * nx:(i + 1) * nx, :] = relay[pl.ds(i, nx, stride=ny), :]
+    goal_got[rows_of(ty, nx), :] = sorted_goal[rows_of(ty, nx), :]
+    launch(1)
+    fill(2)
+    multiply(3)
+    for copy in along_ty:
+        copy.start()
+
     def busy(q):
         launch(q - 2)
         fill(q - 1)
@@ -271,20 +309,22 @@
         launch(q - 2)
         fill(q - 1)
 
-    every(3, groups, busy)
+    every(4, groups, busy)
     every(groups, last + 1, rest)
     launch(last - 1)
 
-    every(1, n, lambda d: meta_copy(d).wait())
-    table = pltpu.make_async_copy(meta_got, meta_smem, local_sem.at[4])
-    table.start()
-    table.wait()
+    for copy in along_ty:
+        copy.wait()
+    goal_table = pltpu.make_async_copy(goal_got, goal_smem, local_sem.at[4])
+    goal_table.start()
+    goal_table.wait()
 
     def add(tiles, d, sums):
         sums = list(sums)
+        source = lax.rem(me + (n - d) * STEP, n)
         for k in range(CAP):
             tile = tiles[d, k]
-            t = meta_smem[d, 0, k]
+            t = goal_smem[source, k]
             for j in range(TBD):
                 sums[j] = sums[j] + jnp.where(t == j, tile, 0.0)
         return tuple(sums)
@@ -332,9 +372,13 @@
             pltpu.VMEM((tall, wide), f32),
             pltpu.VMEM((tall, wide), f32),
             pltpu.VMEM((tall, wide), f32),
-            pltpu.VMEM((rows, 128), f32),
-            pltpu.VMEM((tall, 128), f32),
-            pltpu.VMEM((tall, 128), f32),
+            pltpu.VMEM((8 * FOLD, 128), f32),
+            pltpu.VMEM((8 * FOLD + 16, 128), f32),
+            pltpu.VMEM((8 * FOLD + 16, 128), f32),
+            pltpu.VMEM((24, cols), f32),
+            pltpu.VMEM((24, cols), f32),
+            pltpu.VMEM((24, cols), f32),
+            pltpu.VMEM((24, cols), f32),
             pltpu.VMEM((nvar * rows, 128), f32),
             pltpu.VMEM((nvar * rows, 128), f32),
             pltpu.VMEM((rows // BH * BCOL, NVAR, CELLS), f32),
@@ -345,16 +389,17 @@
             pltpu.VMEM((8, pairs), i32),
             pltpu.SMEM((8, pairs), i32),
             pltpu.VMEM((n, 128), i32),
-            pltpu.VMEM((n, 1, 128), i32),
-            pltpu.VMEM((n, 1, 128), i32),
-            pltpu.SMEM((n, 1, 128), i32),
+            pltpu.VMEM((n, 128), i32),
+            pltpu.VMEM((n, 128), i32),
+            pltpu.VMEM((n, 128), i32),
+            pltpu.SMEM((n, 128), i32),
             sem((5,)),
-            sem((10,)),
-            sem((10,)),
+            sem((8,)),
+            sem((8,)),
             sem((n,)),
             sem((n,)),
-            sem((n,)),
-            sem((n,)),
+            sem((nx + ny,)),
+            sem((nx + ny,)),
             pltpu.SemaphoreType.REGULAR,
         ],
         compiler_params=pltpu.CompilerParams(

time: 55.3 us -> 52.2 us (0.944)
  Pallas kernels: 53.1 us -> 50.5 us
    pallas_call x1, Pallas kernels: 53.1 us -> 50.5 us  [on_device(): pl.pallas_call(functools.partial(kernel, ny, nx), out_shape=jax.ShapeDtyp...]
where the time goes in v3:
time: 52.2 us; the launch traced here: 52 us
  Pallas kernels  50.5 us (97%)
  local copies, waits for them, and re-layouts  1.47 us (3%)
    pallas_call x1, Pallas kernels, on_device(): pl.pallas_call(functools.partial(kernel, ny, nx), out_shape=jax.ShapeDtyp...  50.5 us
    unnamed x1, local copies, waits for them, and re-layouts  1.47 us

profile of v3, /device:TPU:1, one launch (start us, length us, event | category | flops | bytes accessed | tf_op | source)
XLA Modules:
  0.0 52.0 jit_solution(12903014706737993833)
XLA Ops:
  0.0 50.5 %regrid.1 = f32[16,8,128]{2,1,0:T(8,128)} custom-call(f32[8,96,256]{2,1,0:T(8,128)} %fields_ref.1, f32[96,256]{1,0:T(8,128)} %rate_ref.1, f32[96,256]{1,0:T(8,128)} %area_ref.1, s32[1,256]{1,0:T(1,128)} %bitcast.3, s32[1,256]{1,0:T(1,128)} %bitcast.4, s32[1,256]{1,0:T(1,128)} %bitcast.5, bf16[256,128,128]{2,1,0:T(8,128)(2,1)} %weight_ref.1, ...), custom_call_target="tpu_custom_call" | custom-call | tf_op jit(solution)/shard_map/regrid/pallas_call | solution.py:362
  50.5 1.5 %copy.10 = f32[16,8,128]{2,1,0:T(8,128)} copy(f32[16,8,128]{2,1,0:T(8,128)} %regrid.1) | data formatting | bytes 131072

commit v4 on v3

--- a/solution.py
+++ b/solution.py
@@ -20,21 +20,23 @@
 GROUP = 16
 SLOTS = GROUP // CAP
 FOLD = 4
+BATCH = 8
 FORM = 3
 
 
 def kernel(
     ny, nx,
-    fields_ref, rate_ref, area_ref, block_ref, owner_ref, target_ref, weight_ref, target_area_ref,
+    fields_hbm, rate_hbm, area_hbm, block_hbm, owner_hbm, target_hbm, weight_hbm, target_area_hbm,
     out_ref,
+    area_ref, block_ref, owner_ref, target_ref, target_area_ref,
     x, y, rate, k_east, k_west, k_north, k_south, pack, from_west, from_east,
     up, down, from_south, from_north, s0, s1,
     blocks, weights, part, send, got, tables, tables_smem, goal, relay, sorted_goal, goal_got, goal_smem,
     local_sem, edge_send, edge_recv, data_send, data_recv, goal_send, goal_recv, ready,
 ):
     n = ny * nx
-    rows, cols = rate_ref.shape
-    pairs = weight_ref.shape[0]
+    rows, cols = rate_hbm.shape
+    pairs = weight_hbm.shape[0]
     total_rows = rows * ny
     ty, tx = lax.axis_index("ty"), lax.axis_index("tx")
     me = ty * nx + tx
@@ -50,14 +52,21 @@
         pl.semaphore_signal(entry, inc=1, device_id=mate, device_id_type=MESH)
 
     own = slice(8, 8 + rows)
-    load_fields = pltpu.make_async_copy(fields_ref, x.at[:, own, 0:cols], local_sem.at[0])
-    load_rate = pltpu.make_async_copy(rate_ref, rate.at[own, 0:cols], local_sem.at[1])
-    load_weights = pltpu.make_async_copy(weight_ref, weights, local_sem.at[2])
-    load_fields.start()
-    load_rate.start()
-    load_weights.start()
-    load_fields.wait()
-    load_rate.wait()
+    loads = [
+        (fields_hbm, x.at[:, own, 0:cols]),
+        (rate_hbm, rate.at[own, 0:cols]),
+        (block_hbm, block_ref),
+        (owner_hbm, owner_ref),
+        (target_hbm, target_ref),
+        (area_hbm, area_ref),
+        (target_area_hbm, target_area_ref),
+        (weight_hbm, weights),
+    ]
+    loads = [pltpu.make_async_copy(src, dst, local_sem.at[i]) for i, (src, dst) in enumerate(loads)]
+    for load in loads:
+        load.start()
+    for load in loads[:2]:
+        load.wait()
 
     lane = lax.broadcasted_iota(jnp.int32, (8, 128), 1)
     for j in range(FOLD):
@@ -86,21 +95,22 @@
     main, low, high = slice(8, 8 + 8 * FOLD), slice(0, 8), slice(8 + 8 * FOLD, 16 + 8 * FOLD)
     top, bottom = slice(8 * FOLD - 8, 8 * FOLD), slice(0, 8)
     edges = [
-        (pack.at[top], from_west.at[low], corners[0]),
-        (pack.at[top], from_east.at[low], corners[1]),
-        (pack.at[bottom], from_west.at[high], corners[2]),
-        (pack.at[bottom], from_east.at[high], corners[3]),
-        (pack, from_west.at[main], (ty, east)),
-        (pack, from_east.at[main], (ty, west)),
-        (up, from_south, (north, tx)),
-        (down, from_north, (south, tx)),
+        (0, pack.at[top], from_west.at[low], corners[0]),
+        (1, pack.at[top], from_east.at[low], corners[1]),
+        (0, pack.at[bottom], from_west.at[high], corners[2]),
+        (1, pack.at[bottom], from_east.at[high], corners[3]),
+        (0, pack, from_west.at[main], (ty, east)),
+        (1, pack, from_east.at[main], (ty, west)),
+        (2, up, from_south, (north, tx)),
+        (3, down, from_north, (south, tx)),
     ]
-    edges = [edge_copy(i, *edge) for i, edge in enumerate(edges)]
     for edge in edges:
-        edge.start()
+        edge_copy(*edge).start()
     for d in range(1, ny):
         pl.semaphore_signal(ready, inc=1, device_id=(lax.rem(ty + d, ny), tx), device_id_type=MESH)
 
+    for load in loads[2:5]:
+        load.wait()
     p_lane = lax.broadcasted_iota(jnp.int32, (1, pairs), 1)
     p_row = lax.broadcasted_iota(jnp.int32, (pairs, 1), 0)
     key_row = jnp.bitwise_and((owner_ref[...] - me + n) * BACK, n - 1)
@@ -121,7 +131,7 @@
     tables[0:1, :] = jnp.clip(lax.shift_right_logical(joint, 12), 0, pairs - 1)
     tables[1:2, :] = jnp.clip(jnp.bitwise_and(lax.shift_right_logical(joint, 4), 255), 0, blocks.shape[0] - 1)
     tables[2:3, :] = along(0, key_col < p_lane, 1)
-    table_copy = pltpu.make_async_copy(tables, tables_smem, local_sem.at[3])
+    table_copy = pltpu.make_async_copy(tables, tables_smem, local_sem.at[8])
     table_copy.start()
 
     r_col = lax.broadcasted_iota(jnp.int32, (n, 1), 0)
@@ -145,13 +155,13 @@
     along_tx, along_ty = [], []
     for d in range(1, nx):
         to = lax.rem(tx + d, nx)
-        along_tx.append(goal_copy(d, goal.at[rows_of(to, ny)], relay.at[rows_of(tx, ny)], (ty, to)))
+        along_tx.append(goal_copy(0, goal.at[rows_of(to, ny)], relay.at[d * ny:(d + 1) * ny], (ty, to)))
     for d in range(1, ny):
         to = lax.rem(ty + d, ny)
-        along_ty.append(goal_copy(nx + d, sorted_goal.at[rows_of(to, nx)], goal_got.at[rows_of(ty, nx)], (to, tx)))
+        along_ty.append(goal_copy(1, sorted_goal.at[rows_of(to, nx)], goal_got.at[d * nx:(d + 1) * nx], (to, tx)))
     for copy in along_tx:
         copy.start()
-    relay[rows_of(tx, ny), :] = goal[rows_of(tx, ny), :]
+    relay[0:ny, :] = goal[rows_of(tx, ny), :]
 
     def peer(d):
         p = lax.rem(me + lax.rem(d * STEP, n), n)
@@ -159,8 +169,8 @@
 
     def data_copy(d):
         return pltpu.make_async_remote_copy(
-            src_ref=send.at[d], dst_ref=got.at[d], send_sem=data_send.at[d],
-            recv_sem=data_recv.at[d], device_id=peer(d), device_id_type=MESH)
+            src_ref=send.at[d], dst_ref=got.at[d], send_sem=data_send,
+            recv_sem=data_recv.at[lax.div(d, BATCH)], device_id=peer(d), device_id_type=MESH)
 
     def every(start, stop, action):
         def body(d, carry):
@@ -168,8 +178,8 @@
             return carry
         lax.fori_loop(start, stop, body, 0)
 
-    for edge in edges:
-        edge.wait()
+    for i, landed in enumerate((from_west, from_east, from_south, from_north)):
+        edge_copy(i, landed, landed, (ty, east)).wait()
 
     both = []
     for i in range(FOLD + 2):
@@ -237,6 +247,7 @@
             s1[pl.ds(r, 8), :] = z[:, 128:256]
         return carry
 
+    loads[5].wait()
     lax.fori_loop(0, NVAR, smooth, 0)
 
     def form(q, carry):
@@ -259,7 +270,8 @@
     lax.fori_loop(0, rows // BH // FORM, form, 0)
 
     table_copy.wait()
-    load_weights.wait()
+    for load in loads[6:]:
+        load.wait()
 
     def multiply(q):
         for u in range(GROUP):
@@ -289,11 +301,11 @@
     fill(1)
     multiply(2)
 
-    for copy in along_tx:
-        copy.wait()
+    landed = relay.at[ny:n]
+    goal_copy(0, landed, landed, (ty, east)).wait()
     for i in range(ny):
         sorted_goal[i * nx:(i + 1) * nx, :] = relay[pl.ds(i, nx, stride=ny), :]
-    goal_got[rows_of(ty, nx), :] = sorted_goal[rows_of(ty, nx), :]
+    goal_got[0:nx, :] = sorted_goal[rows_of(ty, nx), :]
     launch(1)
     fill(2)
     multiply(3)
@@ -313,29 +325,39 @@
     every(groups, last + 1, rest)
     launch(last - 1)
 
-    for copy in along_ty:
-        copy.wait()
-    goal_table = pltpu.make_async_copy(goal_got, goal_smem, local_sem.at[4])
+    landed = goal_got.at[nx:n]
+    goal_copy(1, landed, landed, (north, tx)).wait()
+    goal_table = pltpu.make_async_copy(goal_got, goal_smem, local_sem.at[9])
     goal_table.start()
     goal_table.wait()
+
+    def arrived(b, start, size):
+        landed = got.at[pl.ds(start, size)]
+        return pltpu.make_async_remote_copy(
+            src_ref=landed, dst_ref=landed, send_sem=data_send, recv_sem=data_recv.at[b],
+            device_id=(ty, east), device_id_type=MESH)
 
     def add(tiles, d, sums):
         sums = list(sums)
         source = lax.rem(me + (n - d) * STEP, n)
+        row = lax.rem(ty + ny - lax.div(source, nx), ny) * nx + lax.rem(tx + nx - lax.rem(source, nx), nx)
         for k in range(CAP):
             tile = tiles[d, k]
-            t = goal_smem[source, k]
+            t = jnp.full((NVAR, CELLS), goal_smem[row, k], jnp.int32)
             for j in range(TBD):
                 sums[j] = sums[j] + jnp.where(t == j, tile, 0.0)
         return tuple(sums)
 
-    def collect(d, sums):
-        data_copy(d).wait()
-        return add(got, d, sums)
+    def collect(b, sums):
+        arrived(b, b * BATCH, BATCH).wait_recv()
+        return lax.fori_loop(b * BATCH, (b + 1) * BATCH, functools.partial(add, got), sums)
 
     zero = jnp.zeros((NVAR, CELLS), jnp.float32)
     sums = add(send, 0, (zero,) * TBD)
-    sums = lax.fori_loop(1, n, collect, sums)
+    arrived(0, 1, BATCH - 1).wait_recv()
+    sums = lax.fori_loop(1, BATCH, functools.partial(add, got), sums)
+    sums = lax.fori_loop(1, n // BATCH, collect, sums)
+    arrived(0, 1, n - 1).wait_send()
     for j in range(TBD):
         out_ref[j] = sums[j] / target_area_ref[j:j + 1, :]
 
@@ -362,9 +384,14 @@
     return pl.pallas_call(
         functools.partial(kernel, ny, nx),
         out_shape=jax.ShapeDtypeStruct((TBD, NVAR, CELLS), f32),
-        in_specs=[hbm, hbm, vmem, vmem, vmem, vmem, hbm, vmem],
+        in_specs=[hbm] * 8,
         out_specs=vmem,
         scratch_shapes=[
+            pltpu.VMEM((rows, cols), f32),
+            pltpu.VMEM((1, pairs), i32),
+            pltpu.VMEM((1, pairs), i32),
+            pltpu.VMEM((1, pairs), i32),
+            pltpu.VMEM((TBD, CELLS), f32),
             pltpu.VMEM((nvar, tall, wide), f32),
             pltpu.VMEM((nvar, tall, wide), f32),
             pltpu.VMEM((tall, wide), f32),
@@ -393,13 +420,13 @@
             pltpu.VMEM((n, 128), i32),
             pltpu.VMEM((n, 128), i32),
             pltpu.SMEM((n, 128), i32),
-            sem((5,)),
-            sem((8,)),
-            sem((8,)),
-            sem((n,)),
-            sem((n,)),
-            sem((nx + ny,)),
-            sem((nx + ny,)),
+            sem((10,)),
+            sem((4,)),
+            sem((4,)),
+            sem,
+            sem((n // BATCH,)),
+            sem((2,)),
+            sem((2,)),
             pltpu.SemaphoreType.REGULAR,
         ],
         compiler_params=pltpu.CompilerParams(

time: 52.2 us -> 48.2 us (0.923)
  Pallas kernels: 50.5 us -> 46.5 us
    pallas_call x1, Pallas kernels: 50.5 us -> 46.5 us  [on_device(): pl.pallas_call(functools.partial(kernel, ny, nx), out_shape=jax.ShapeDtyp...]
where the time goes in v4:
time: 48.2 us; the launch traced here: 48 us
  Pallas kernels  46.5 us (96%)
  local copies, waits for them, and re-layouts  1.47 us (3%)
    pallas_call x1, Pallas kernels, on_device(): pl.pallas_call(functools.partial(kernel, ny, nx), out_shape=jax.ShapeDtyp...  46.5 us
    unnamed x1, local copies, waits for them, and re-layouts  1.47 us

profile of v4, /device:TPU:1, one launch (start us, length us, event | category | flops | bytes accessed | tf_op | source)
XLA Modules:
  0.0 48.0 jit_solution(6757302620931480058)
XLA Ops:
  0.0 46.5 %regrid.1 = f32[16,8,128]{2,1,0:T(8,128)} custom-call(f32[8,96,256]{2,1,0:T(8,128)} %fields_hbm.1, f32[96,256]{1,0:T(8,128)} %rate_hbm.1, f32[96,256]{1,0:T(8,128)} %area_hbm.1, s32[1,256]{1,0:T(1,128)} %bitcast.3, s32[1,256]{1,0:T(1,128)} %bitcast.4, s32[1,256]{1,0:T(1,128)} %bitcast.5, bf16[256,128,128]{2,1,0:T(8,128)(2,1)} %weight_hbm.1, ...), custom_call_target="tpu_custom_call" | custom-call | tf_op jit(solution)/shard_map/regrid/pallas_call | solution.py:384
  46.5 1.5 %copy.10 = f32[16,8,128]{2,1,0:T(8,128)} copy(f32[16,8,128]{2,1,0:T(8,128)} %regrid.1) | data formatting | bytes 131072

commit v5 on v4

v5 whole, which is shorter than its diff:
```python
import functools

import jax
import jax.numpy as jnp
from jax import lax
from jax.experimental import pallas as pl
from jax.experimental.pallas import tpu as pltpu
from jax.sharding import PartitionSpec as P

NVAR = 8
BH = 8
BW = 16
BR = 12
BCOL = 16
TBD = 16
CAP = 4
CELLS = BH * BW
MESH = pl.DeviceIdType.MESH
STEP, BACK = 51, 123
GROUP = 16
SLOTS = GROUP // CAP
FOLD = 32
BATCH = 8
FIRST = 14
SECOND = 2
SIDE_FIRST, SIDE_SECOND = 49, 6


def kernel(
    ny, nx,
    fields_hbm, rate_hbm, area_hbm, block_hbm, owner_hbm, target_hbm, weight_hbm, target_area_hbm,
    out_ref,
    area_ref, block_ref, owner_ref, target_ref, target_area_ref,
    area_sides, stage, x0, x1, xe, y0, y1, ye, rate, k_east, k_north, pack, from_west, from_east,
    blocks, weights, part, send, got, tables, tables_smem, goal, relay, sorted_goal, goal_got, goal_smem,
    local_sem, edge_send, edge_recv, data_send, data_recv, goal_send, goal_recv, ready,
):
    n = ny * nx
    rows, cols = rate_hbm.shape
    pairs = weight_hbm.shape[0]
    total_rows = rows * ny
    ty, tx = lax.axis_index("ty"), lax.axis_index("tx")
    me = ty * nx + tx
    north, south = lax.rem(ty + 1, ny), lax.rem(ty + ny - 1, ny)
    east, west = lax.rem(tx + 1, nx), lax.rem(tx + nx - 1, nx)
    corners = [(north, east), (north, west), (south, east), (south, west)]

    entry = pltpu.get_barrier_semaphore()
    mates = [(ty, lax.rem(tx + d, nx)) for d in range(1, nx)]
    mates += [(lax.rem(ty + d, ny), tx) for d in range(1, ny)]
    mates += corners
    for mate in mates:
        pl.semaphore_signal(entry, inc=1, device_id=mate, device_id_type=MESH)

    own = slice(8, 8 + rows)
    loads = [
        (fields_hbm, stage),
        (rate_hbm.at[:, 0:128], rate.at[0, own]),
        (rate_hbm.at[:, 128:256], rate.at[1, own]),
        (block_hbm, block_ref),
        (owner_hbm, owner_ref),
        (target_hbm, target_ref),
        (area_hbm.at[:, 0:128], area_ref.at[0]),
        (area_hbm.at[:, 128:256], area_ref.at[1]),
        (target_area_hbm, target_area_ref),
        (weight_hbm, weights),
    ]
    loads = [pltpu.make_async_copy(src, dst, local_sem.at[i]) for i, (src, dst) in enumerate(loads)]
    for load in loads:
        load.start()
    for load in loads[:3]:
        load.wait()

    lane = lax.broadcasted_iota(jnp.int32, (8, 128), 1)
    xs, ys = (x0, x1), (y0, y1)

    def row(field, r):
        return field[pl.ds(pl.multiple_of(r * NVAR, NVAR), NVAR), :]

    def turn(i, carry):
        for v in range(NVAR):
            for t in range(2):
                tile = stage[v, pl.ds(pl.multiple_of(8 * i, 8), 8), 128 * t:128 * t + 128]
                xs[t][pl.ds((8 + 8 * i) * NVAR + v, 8, stride=NVAR), :] = tile
        return carry

    lax.fori_loop(0, rows // 8, turn, 0)

    def packed(firsts, lasts):
        total = jnp.zeros((8, 128), jnp.float32)
        for j, (first, last) in enumerate(zip(firsts, lasts)):
            edge = pltpu.roll(jnp.where(lane < 64, first, last), 4 * j + 2, 1)
            total = jnp.where((lane >= 4 * j) & (lane < 4 * j + 4), edge, total)
        return total

    for g, place in enumerate((0, 3, 2)):
        group = range(8 + FOLD * g, 8 + FOLD * (g + 1))
        pack[place] = packed([row(x0, r) for r in group], [row(x1, r) for r in group])
    group = range(8, 8 + rows, 8)
    pack[1] = packed([rate[0, r:r + 8, :] for r in group], [rate[1, r:r + 8, :] for r in group])

    pl.semaphore_wait(entry, len(mates))

    def edge_copy(i, src, dst, device):
        return pltpu.make_async_remote_copy(
            src_ref=src, dst_ref=dst, send_sem=edge_send.at[i], recv_sem=edge_recv.at[i],
            device_id=device, device_id_type=MESH)

    low, high = slice(6 * NVAR, 8 * NVAR), slice((8 + rows) * NVAR, (10 + rows) * NVAR)
    top, bottom = slice((6 + rows) * NVAR, (8 + rows) * NVAR), slice(8 * NVAR, 10 * NVAR)
    rate_low, rate_high = rate.at[0:2, 0:8], rate.at[0:2, 8 + rows:16 + rows]
    edges = [
        (0, pack.at[1:3], from_west.at[4:6], corners[0]),
        (1, pack.at[1:3], from_east.at[4:6], corners[1]),
        (0, pack.at[0:2], from_west.at[6:8], corners[2]),
        (1, pack.at[0:2], from_east.at[6:8], corners[3]),
        (0, pack, from_west.at[0:4], (ty, east)),
        (1, pack, from_east.at[0:4], (ty, west)),
        (2, x0.at[top], x0.at[low], (north, tx)),
        (3, x1.at[top], x1.at[low], (north, tx)),
        (4, rate.at[0:2, rows:8 + rows], rate_low, (north, tx)),
        (5, x0.at[bottom], x0.at[high], (south, tx)),
        (6, x1.at[bottom], x1.at[high], (south, tx)),
        (7, rate.at[0:2, 8:16], rate_high, (south, tx)),
    ]
    for edge in edges:
        edge_copy(*edge).start()
    for d in range(1, ny):
        pl.semaphore_signal(ready, inc=1, device_id=(lax.rem(ty + d, ny), tx), device_id_type=MESH)

    for load in loads[3:6]:
        load.wait()
    p_lane = lax.broadcasted_iota(jnp.int32, (1, pairs), 1)
    p_row = lax.broadcasted_iota(jnp.int32, (pairs, 1), 0)
    key_row = jnp.bitwise_and((owner_ref[...] - me + n) * BACK, n - 1)
    joint_row = p_lane * 4096 + block_ref[...] * TBD + target_ref[...]
    goal_row = target_ref[...] + 1
    eye = lax.broadcasted_iota(jnp.int32, (pairs, pairs), 0) == lax.broadcasted_iota(jnp.int32, (pairs, pairs), 1)

    def along(axis, mask, value):
        return jnp.sum(jnp.where(mask, value, 0), axis=axis, keepdims=True, dtype=jnp.int32)

    unique_row = key_row * pairs + p_lane
    key_col = along(1, eye, key_row)
    joint_col = along(1, eye, joint_row)
    unique_col = key_col * pairs + p_row
    place_row = along(0, unique_col < unique_row, 1)
    place_col = along(1, unique_row < unique_col, 1)
    joint = along(0, place_col == p_lane, joint_col)
    tables[0:1, :] = jnp.clip(lax.shift_right_logical(joint, 12), 0, pairs - 1)
    tables[1:2, :] = jnp.clip(jnp.bitwise_and(lax.shift_right_logical(joint, 4), 255), 0, blocks.shape[0] - 1)
    tables[2:3, :] = along(0, key_col < p_lane, 1)
    table_copy = pltpu.make_async_copy(tables, tables_smem, local_sem.at[10])
    table_copy.start()

    r_col = lax.broadcasted_iota(jnp.int32, (n, 1), 0)
    owner_col = lax.rem(r_col, ny) * nx + lax.div(r_col, ny)
    d_col = jnp.bitwise_and((owner_col - me + n) * BACK, n - 1)
    rank = jnp.where(key_row == d_col, place_row - along(1, key_row < d_col, 1), -1)
    d_lane = lax.broadcasted_iota(jnp.int32, (n, 128), 1)
    goals = jnp.zeros((n, 128), jnp.int32)
    for k in range(CAP):
        goals = jnp.where(d_lane == k, along(1, rank == k, goal_row), goals)
    goal[...] = goals - 1

    def rows_of(i, size):
        return pl.ds(pl.multiple_of(i * size, 8), size)

    def goal_copy(i, src, dst, device):
        return pltpu.make_async_remote_copy(
            src_ref=src, dst_ref=dst, send_sem=goal_send.at[i], recv_sem=goal_recv.at[i],
            device_id=device, device_id_type=MESH)

    along_tx, along_ty = [], []
    for d in range(1, nx):
        to = lax.rem(tx + d, nx)
        along_tx.append(goal_copy(0, goal.at[rows_of(to, ny)], relay.at[d * ny:(d + 1) * ny], (ty, to)))
    for d in range(1, ny):
        to = lax.rem(ty + d, ny)
        along_ty.append(goal_copy(1, sorted_goal.at[rows_of(to, nx)], goal_got.at[d * nx:(d + 1) * nx], (to, tx)))
    for copy in along_tx:
        copy.start()
    relay[0:ny, :] = goal[rows_of(tx, ny), :]

    sub = lax.broadcasted_iota(jnp.int32, (8, 128), 0)
    inner = (rows + 8) // 8
    bands = inner + 1

    def from_next(tiles):
        moved = [pltpu.roll(c, 127, 1) for c in tiles]
        if len(tiles) == 1:
            return moved
        return [jnp.where(lane < 127, moved[t], moved[1 - t]) for t in range(2)]

    def from_previous(tiles):
        moved = [pltpu.roll(c, 1, 1) for c in tiles]
        if len(tiles) == 1:
            return moved
        return [jnp.where(lane > 0, moved[t], moved[1 - t]) for t in range(2)]

    def rate_band(tiles, i, last):
        here, above = [[rate[t, 8 * b:8 * b + 8, :] for t in tiles] for b in (i, min(i + 1, last))]
        g = sub + (ty * rows + 8 * i - 8)
        inside = (g >= 0) & (g < total_rows - 1)
        for t, c, n_value, e in zip(tiles, here, above, from_next(here)):
            n_value = jnp.where(sub < 7, pltpu.roll(c, 7, 0), pltpu.roll(n_value, 7, 0))
            k_east[t, 8 * i:8 * i + 8, :] = 0.5 * (c + e)
            k_north[t, 8 * i:8 * i + 8, :] = jnp.where(inside, 0.5 * (c + n_value), 0.0)

    def north_flux(t, r, c, n_value):
        return k_north[t, pl.ds(r, 1), :] * (n_value - c)

    def advance(fields, tiles, r, c, below):
        above = [row(field, r + 1) for field in fields]
        flux = [north_flux(t, r, *pair) for t, pair in zip(tiles, zip(c, above))]
        side = [k_east[t, pl.ds(r, 1), :] * (e - p) for t, p, e in zip(tiles, c, from_next(c))]
        back = from_previous(side)
        return above, flux, [p + a - b + f - q for p, a, b, f, q in zip(c, side, back, flux, below)]

    def begin_at(fields, tiles, r):
        c = [row(field, r) for field in fields]
        return c, [north_flux(t, r - 1, row(field, r - 1), p) for t, field, p in zip(tiles, fields, c)]

    def first_pass(fields, results, tiles, start, count, carry):
        for u in range(count):
            *carry, z = advance(fields, tiles, start + u, *carry)
            for result, p in zip(results, z):
                result[pl.ds(pl.multiple_of((start + u) * NVAR, NVAR), NVAR), :] = p
        return tuple(carry)

    def second_pass(fields, tiles, block, carry):
        out = []
        for j in range(BH):
            *carry, z = advance(fields, tiles, 8 + block * BH + j, *carry)
            out.append(z)
        return tuple(carry), out

    def whole_blocks(block, carry):
        carry, out = second_pass(ys, (0, 1), block, carry)
        for t in range(2):
            tile = [area_ref[t, pl.ds(block * BH + j, 1), :] * z[t] for j, z in enumerate(out)]
            for bit in (1, 2, 4):
                mask = jnp.bitwise_and(lane, 16 * bit) == 0
                for j in range(BH):
                    if j & bit:
                        continue
                    lo, hi = tile[j], tile[j + bit]
                    tile[j] = jnp.where(mask, lo, pltpu.roll(hi, 16 * bit, 1))
                    tile[j + bit] = jnp.where(mask, pltpu.roll(lo, 128 - 16 * bit, 1), hi)
            for j in range(BH):
                blocks[block * BCOL + t * BH + j] = tile[j]
        return carry

    for i in range(1, inner):
        rate_band((0, 1), i, inner - 1)
    block_rows = rows // BH
    every_row = lambda r: jnp.where(lane < 60, row(x0, r), pltpu.roll(row(x1, r), 124, 1))

    def inside_first(b, carry):
        for u in range(FIRST):
            r = 14 + b * FIRST + u
            xe[pl.ds(pl.multiple_of(r * NVAR, NVAR), NVAR), :] = every_row(r)
        return first_pass(xs, ys, (0, 1), 14 + b * FIRST, FIRST, carry)

    lax.fori_loop(0, (rows - 12) // FIRST, inside_first, begin_at(xs, (0, 1), 14))
    for load in loads[6:8]:
        load.wait()

    def inside_second(b, carry):
        for u in range(SECOND):
            carry = whole_blocks(1 + b * SECOND + u, carry)
        return carry

    lax.fori_loop(0, (block_rows - 2) // SECOND, inside_second, begin_at(ys, (0, 1), 16))

    for block in range(block_rows):
        for t, base in enumerate((0, 112)):
            total = jnp.zeros((1, 128), jnp.float32)
            for j in range(BH):
                moved = pltpu.roll(jnp.broadcast_to(area_ref[t, block * BH + j:block * BH + j + 1, :], (8, 128)), (16 * j - base) % 128, 1)
                total = jnp.where(lax.shift_right_logical(lane[0:1], 4) == j, moved[0:1], total)
            area_sides[t, block:block + 1, :] = total

    landing = (from_west, from_east, x0.at[low], x1.at[low], rate_low, x0.at[high], x1.at[high], rate_high)
    for i, landed in enumerate(landing):
        edge_copy(i, landed, landed, (ty, east)).wait()

    for i in (0, inner - 1, inner):
        rate_band((0, 1), i, inner)

    def ends(side, carry):
        start = 7 + side * (rows - 5)
        first_pass(xs, ys, (0, 1), start, 7, begin_at(xs, (0, 1), start))
        return carry

    ends(0, 0)
    ends(1, 0)

    def end_blocks(side, carry):
        block = side * (block_rows - 1)
        whole_blocks(block, begin_at(ys, (0, 1), 8 + block * BH))
        return carry

    end_blocks(0, 0)
    end_blocks(1, 0)

    both = []
    for i in range(8):
        both.append(jnp.where(jnp.bitwise_and(lane, 3) < 2, pltpu.roll(from_east[i], 126, 1), pltpu.roll(from_west[i], 2, 1)))

    def opened(tile, j):
        return pltpu.roll(tile, 124 - 4 * j, 1) if j < 31 else tile

    def put(r, tile, j):
        own_part = xe[NVAR * r:NVAR * r + NVAR, :] if 14 <= r < 2 + rows else every_row(r)
        xe[NVAR * r:NVAR * r + NVAR, :] = jnp.where(lane < 124, own_part, opened(tile, j))

    for g, place in enumerate((0, 3, 2)):
        for j in range(FOLD):
            put(8 + FOLD * g + j, both[place], j)
    put(7, both[5], FOLD - 1)
    put(8 + rows, both[6], 0)
    for r in (6, 9 + rows):
        xe[NVAR * r:NVAR * r + NVAR, :] = every_row(r)
    for i in range(bands):
        if i == 0:
            side = opened(both[4], rows // 8 - 1)
        elif i == inner:
            side = opened(both[7], 0)
        else:
            side = opened(both[1], i - 1)
        own_part = jnp.where(lane < 60, rate[0, 8 * i:8 * i + 8, :], pltpu.roll(rate[1, 8 * i:8 * i + 8, :], 124, 1))
        rate[2, 8 * i:8 * i + 8, :] = jnp.where(lane < 124, own_part, side)
    for i in range(bands):
        rate_band((2,), i, inner)

    def side_first(b, carry):
        return first_pass((xe,), (ye,), (2,), 7 + b * SIDE_FIRST, SIDE_FIRST, carry)

    lax.fori_loop(0, (rows + 2) // SIDE_FIRST, side_first, begin_at((xe,), (2,), 7))

    def side_second(b, carry):
        for u in range(SIDE_SECOND):
            block = b * SIDE_SECOND + u
            carry, out = second_pass((ye,), (2,), block, carry)
            left, right = None, None
            for j, (z,) in enumerate(out):
                l_value = pltpu.roll(z, 16 * j, 1) if j else z
                r_value = pltpu.roll(z, (16 * j + 20) % 128, 1)
                here = lax.shift_right_logical(lane, 4) == j
                left = l_value if j == 0 else jnp.where(here, l_value, left)
                right = r_value if j == 0 else jnp.where(here, r_value, right)
            blocks[block * BCOL] = left * area_sides[0, pl.ds(block, 1), :]
            blocks[block * BCOL + BCOL - 1] = right * area_sides[1, pl.ds(block, 1), :]
        return carry

    lax.fori_loop(0, block_rows // SIDE_SECOND, side_second, begin_at((ye,), (2,), 8))

    def peer(d):
        p = lax.rem(me + lax.rem(d * STEP, n), n)
        return (p // nx, lax.rem(p, nx))

    def data_copy(d):
        return pltpu.make_async_remote_copy(
            src_ref=send.at[d], dst_ref=got.at[d], send_sem=data_send,
            recv_sem=data_recv.at[lax.div(d, BATCH)], device_id=peer(d), device_id_type=MESH)

    def every(start, stop, action):
        def body(d, carry):
            action(d)
            return carry
        lax.fori_loop(start, stop, body, 0)

    table_copy.wait()
    for load in loads[8:]:
        load.wait()

    def multiply(q):
        for u in range(GROUP):
            i = q * GROUP + u
            a = blocks[tables_smem[1, i]].astype(jnp.bfloat16)
            part[i] = jnp.dot(a, weights[tables_smem[0, i]], preferred_element_type=jnp.float32)

    def fill(q):
        for u in range(SLOTS):
            d = q * SLOTS + u
            first = tables_smem[2, d]
            for k in range(CAP):
                send[d, k] = part[jnp.minimum(first + k, pairs - 1)]

    def launch(q):
        for u in range(SLOTS):
            data_copy(q * SLOTS + u).start()

    last = n // SLOTS
    groups = pairs // GROUP
    multiply(0)
    fill(0)
    multiply(1)
    pl.semaphore_wait(ready, ny - 1)
    for u in range(1, SLOTS):
        data_copy(u).start()
    fill(1)
    multiply(2)

    landed = relay.at[ny:n]
    goal_copy(0, landed, landed, (ty, east)).wait()
    for i in range(ny):
        sorted_goal[i * nx:(i + 1) * nx, :] = relay[pl.ds(i, nx, stride=ny), :]
    goal_got[0:nx, :] = sorted_goal[rows_of(ty, nx), :]
    launch(1)
    fill(2)
    multiply(3)
    for copy in along_ty:
        copy.start()

    def busy(q):
        launch(q - 2)
        fill(q - 1)
        multiply(q)

    def rest(q):
        launch(q - 2)
        fill(q - 1)

    every(4, groups, busy)
    every(groups, last + 1, rest)
    launch(last - 1)

    landed = goal_got.at[nx:n]
    goal_copy(1, landed, landed, (north, tx)).wait()
    goal_table = pltpu.make_async_copy(goal_got, goal_smem, local_sem.at[11])
    goal_table.start()
    goal_table.wait()

    def arrived(b, start, size):
        landed = got.at[pl.ds(start, size)]
        return pltpu.make_async_remote_copy(
            src_ref=landed, dst_ref=landed, send_sem=data_send, recv_sem=data_recv.at[b],
            device_id=(ty, east), device_id_type=MESH)

    def add(tiles, d, sums):
        sums = list(sums)
        source = lax.rem(me + (n - d) * STEP, n)
        row = lax.rem(ty + ny - lax.div(source, nx), ny) * nx + lax.rem(tx + nx - lax.rem(source, nx), nx)
        for k in range(CAP):
            tile = tiles[d, k]
            t = jnp.full((NVAR, CELLS), goal_smem[row, k], jnp.int32)
            for j in range(TBD):
                sums[j] = sums[j] + jnp.where(t == j, tile, 0.0)
        return tuple(sums)

    def collect(b, sums):
        arrived(b, b * BATCH, BATCH).wait_recv()
        return lax.fori_loop(b * BATCH, (b + 1) * BATCH, functools.partial(add, got), sums)

    zero = jnp.zeros((NVAR, CELLS), jnp.float32)
    sums = add(send, 0, (zero,) * TBD)
    arrived(0, 1, BATCH - 1).wait_recv()
    sums = lax.fori_loop(1, BATCH, functools.partial(add, got), sums)
    sums = lax.fori_loop(1, n // BATCH, collect, sums)
    arrived(0, 1, n - 1).wait_send()
    for j in range(TBD):
        out_ref[j] = sums[j] / target_area_ref[j:j + 1, :]


def on_device(
    ny, nx,
    source_fields,
    diffusivity,
    cell_area,
    pair_block,
    pair_owner,
    pair_target,
    weight_blocks,
    target_area,
):
    n = ny * nx
    nvar, rows, cols = source_fields.shape
    pairs = weight_blocks.shape[0]
    vmem = pl.BlockSpec(memory_space=pltpu.VMEM)
    hbm = pl.BlockSpec(memory_space=pltpu.HBM)
    f32, i32 = jnp.float32, jnp.int32
    tall = rows + 16
    sem = pltpu.SemaphoreType.DMA
    return pl.pallas_call(
        functools.partial(kernel, ny, nx),
        out_shape=jax.ShapeDtypeStruct((TBD, NVAR, CELLS), f32),
        in_specs=[hbm] * 8,
        out_specs=vmem,
        scratch_shapes=[
            pltpu.VMEM((2, rows, 128), f32),
            pltpu.VMEM((1, pairs), i32),
            pltpu.VMEM((1, pairs), i32),
            pltpu.VMEM((1, pairs), i32),
            pltpu.VMEM((TBD, CELLS), f32),
            pltpu.VMEM((2, 16, 128), f32),
            pltpu.VMEM((nvar, rows, cols), f32),
            pltpu.VMEM((tall * nvar, 128), f32),
            pltpu.VMEM((tall * nvar, 128), f32),
            pltpu.VMEM((tall * nvar, 128), f32),
            pltpu.VMEM((tall * nvar, 128), f32),
            pltpu.VMEM((tall * nvar, 128), f32),
            pltpu.VMEM((tall * nvar, 128), f32),
            pltpu.VMEM((3, tall, 128), f32),
            pltpu.VMEM((3, tall, 128), f32),
            pltpu.VMEM((3, tall, 128), f32),
            pltpu.VMEM((4, 8, 128), f32),
            pltpu.VMEM((8, 8, 128), f32),
            pltpu.VMEM((8, 8, 128), f32),
            pltpu.VMEM((rows // BH * BCOL, NVAR, CELLS), f32),
            pltpu.VMEM((pairs, CELLS, CELLS), jnp.bfloat16),
            pltpu.VMEM((pairs, NVAR, CELLS), f32),
            pltpu.VMEM((n, CAP, NVAR, CELLS), f32),
            pltpu.VMEM((n, CAP, NVAR, CELLS), f32),
            pltpu.VMEM((8, pairs), i32),
            pltpu.SMEM((8, pairs), i32),
            pltpu.VMEM((n, 128), i32),
            pltpu.VMEM((n, 128), i32),
            pltpu.VMEM((n, 128), i32),
            pltpu.VMEM((n, 128), i32),
            pltpu.SMEM((n, 128), i32),
            sem((12,)),
            sem((8,)),
            sem((8,)),
            sem,
            sem((n // BATCH,)),
            sem((2,)),
            sem((2,)),
            pltpu.SemaphoreType.REGULAR,
        ],
        compiler_params=pltpu.CompilerParams(
            collective_id=0, has_side_effects=True, vmem_limit_bytes=62 * 1024 * 1024),
        name="regrid",
    )(
        source_fields, diffusivity, cell_area, pair_block.reshape(1, pairs), pair_owner.reshape(1, pairs),
        pair_target.reshape(1, pairs), weight_blocks, target_area,
    )


def solution(mesh):
    return jax.shard_map(
        functools.partial(on_device, mesh.shape["ty"], mesh.shape["tx"]),
        mesh=mesh,
        in_specs=(
            P(None, "ty", "tx"),
            P("ty", "tx"),
            P("ty", "tx"),
            P(("ty", "tx")),
            P(("ty", "tx"), None),
            P(("ty", "tx")),
            P(("ty", "tx"), None, None),
            P(("ty", "tx"), None),
        ),
        out_specs=P(("ty", "tx"), None, None),
        check_vma=False,
    )
```

time: 48.2 us -> 45.7 us (0.948)
  Pallas kernels: 46.5 us -> 44 us
    pallas_call x1, Pallas kernels: 46.5 us -> 44 us  [on_device(): pl.pallas_call(functools.partial(kernel, ny, nx), out_shape=jax.ShapeDtyp...]
where the time goes in v5:
time: 45.7 us; the launch traced here: 45.5 us
  Pallas kernels  44 us (96%)
  local copies, waits for them, and re-layouts  1.47 us (3%)
    pallas_call x1, Pallas kernels, on_device(): pl.pallas_call(functools.partial(kernel, ny, nx), out_shape=jax.ShapeDtyp...  44 us
    unnamed x1, local copies, waits for them, and re-layouts  1.47 us

profile of v5, /device:TPU:1, one launch (start us, length us, event | category | flops | bytes accessed | tf_op | source)
XLA Modules:
  0.0 45.5 jit_solution(17206954376561399804)
XLA Ops:
  0.0 44.0 %regrid.1 = f32[16,8,128]{2,1,0:T(8,128)} custom-call(f32[8,96,256]{2,1,0:T(8,128)} %fields_hbm.1, f32[96,256]{1,0:T(8,128)} %rate_hbm.1, f32[96,256]{1,0:T(8,128)} %area_hbm.1, s32[1,256]{1,0:T(1,128)} %bitcast.3, s32[1,256]{1,0:T(1,128)} %bitcast.4, s32[1,256]{1,0:T(1,128)} %bitcast.5, bf16[256,128,128]{2,1,0:T(8,128)(2,1)} %weight_hbm.1, ...), custom_call_target="tpu_custom_call" | custom-call | tf_op jit(solution)/shard_map/regrid/pallas_call | solution.py:486
  44.1 1.5 %copy.10 = f32[16,8,128]{2,1,0:T(8,128)} copy(f32[16,8,128]{2,1,0:T(8,128)} %regrid.1) | data formatting | bytes 131072

commit v6 on v5

--- a/solution.py
+++ b/solution.py
@@ -16,7 +16,7 @@
 CAP = 4
 CELLS = BH * BW
 MESH = pl.DeviceIdType.MESH
-STEP, BACK = 51, 123
+STEP, BACK = 43, 3
 GROUP = 16
 SLOTS = GROUP // CAP
 FOLD = 32

time: 45.7 us -> 44.8 us (0.980)
  Pallas kernels: 44 us -> 43.1 us
    pallas_call x1, Pallas kernels: 44 us -> 43.1 us  [on_device(): pl.pallas_call(functools.partial(kernel, ny, nx), out_shape=jax.ShapeDtyp...]
where the time goes in v6:
time: 44.8 us; the launch traced here: 44.6 us
  Pallas kernels  43.1 us (96%)
  local copies, waits for them, and re-layouts  1.47 us (3%)
    pallas_call x1, Pallas kernels, on_device(): pl.pallas_call(functools.partial(kernel, ny, nx), out_shape=jax.ShapeDtyp...  43.1 us
    unnamed x1, local copies, waits for them, and re-layouts  1.47 us

profile of v6, /device:TPU:1, one launch (start us, length us, event | category | flops | bytes accessed | tf_op | source)
XLA Modules:
  0.0 44.6 jit_solution(7637535187001475109)
XLA Ops:
  0.0 43.1 %regrid.1 = f32[16,8,128]{2,1,0:T(8,128)} custom-call(f32[8,96,256]{2,1,0:T(8,128)} %fields_hbm.1, f32[96,256]{1,0:T(8,128)} %rate_hbm.1, f32[96,256]{1,0:T(8,128)} %area_hbm.1, s32[1,256]{1,0:T(1,128)} %bitcast.3, s32[1,256]{1,0:T(1,128)} %bitcast.4, s32[1,256]{1,0:T(1,128)} %bitcast.5, bf16[256,128,128]{2,1,0:T(8,128)(2,1)} %weight_hbm.1, ...), custom_call_target="tpu_custom_call" | custom-call | tf_op jit(solution)/shard_map/regrid/pallas_call | solution.py:486
  43.2 1.5 %copy.10 = f32[16,8,128]{2,1,0:T(8,128)} copy(f32[16,8,128]{2,1,0:T(8,128)} %regrid.1) | data formatting | bytes 131072

commit v7 on v6

--- a/solution.py
+++ b/solution.py
@@ -66,10 +66,11 @@
         (weight_hbm, weights),
     ]
     loads = [pltpu.make_async_copy(src, dst, local_sem.at[i]) for i, (src, dst) in enumerate(loads)]
-    for load in loads:
+    for load in loads[:-1]:
         load.start()
     for load in loads[:3]:
         load.wait()
+    loads[-1].start()
 
     lane = lax.broadcasted_iota(jnp.int32, (8, 128), 1)
     xs, ys = (x0, x1), (y0, y1)

time: 44.8 us -> 44.8 us (level)
  no operation moved by 1% of the time
where the time goes in v7:
time: 44.8 us; the launch traced here: 44.6 us
  Pallas kernels  43.1 us (96%)
  local copies, waits for them, and re-layouts  1.47 us (3%)
    pallas_call x1, Pallas kernels, on_device(): pl.pallas_call(functools.partial(kernel, ny, nx), out_shape=jax.ShapeDtyp...  43.1 us
    unnamed x1, local copies, waits for them, and re-layouts  1.47 us

profile of v7, /device:TPU:1, one launch (start us, length us, event | category | flops | bytes accessed | tf_op | source)
XLA Modules:
  0.0 44.6 jit_solution(12223800138385174140)
XLA Ops:
  0.0 43.1 %regrid.1 = f32[16,8,128]{2,1,0:T(8,128)} custom-call(f32[8,96,256]{2,1,0:T(8,128)} %fields_hbm.1, f32[96,256]{1,0:T(8,128)} %rate_hbm.1, f32[96,256]{1,0:T(8,128)} %area_hbm.1, s32[1,256]{1,0:T(1,128)} %bitcast.3, s32[1,256]{1,0:T(1,128)} %bitcast.4, s32[1,256]{1,0:T(1,128)} %bitcast.5, bf16[256,128,128]{2,1,0:T(8,128)(2,1)} %weight_hbm.1, ...), custom_call_target="tpu_custom_call" | custom-call | tf_op jit(solution)/shard_map/regrid/pallas_call | solution.py:487
  43.2 1.5 %copy.10 = f32[16,8,128]{2,1,0:T(8,128)} copy(f32[16,8,128]{2,1,0:T(8,128)} %regrid.1) | data formatting | bytes 131072
